TPU v7x, 32 devices: a whole 2x2x4 slice. The times are simulated.
32 devices in a mesh: dp: 8 (over z, x), seq: 4 (over y, core).
Axes of the slice: x: 2, y: 2, z: 4, core: 2. Of those that a mesh axis runs over, the one named last changes fastest.
Arguments:
- tokens: bfloat16 [2, 8, 1024, 1536], P(None, 'dp', 'seq'), may hold values from -6 to 6
- query_weight: bfloat16 [1536, 768], P('dp'), may hold values from -0.01953125 to 0.01953125
- key_weight: bfloat16 [1536, 768], P('dp'), may hold values from -0.15625 to 0.15625
- value_weight: bfloat16 [1536, 768], P('dp'), may hold values from -0.15625 to 0.15625
- mix_weight: bfloat16 [768, 1536], P('dp'), may hold values from -6 to 6
- gate_weight: bfloat16 [1536, 3968], P('dp'), may hold values from -0.15625 to 0.15625
- up_weight: bfloat16 [1536, 3968], P('dp'), may hold values from -0.15625 to 0.15625
- down_weight: bfloat16 [3968, 1536], P('dp'), may hold values from -0.09375 to 0.09375
- attn_gain: bfloat16 [1536], P('dp'), may hold values from 0.5 to 1.5
- ffn_gain: bfloat16 [1536], P('dp'), may hold values from 0.5 to 1.5
- bias_table: float32 [32, 12], P(None, 'seq'), may hold values from -4 to 4
- bucket_ids: int32 [2048], replicated, may hold values from 0 to 31, as said below
- out_grad: bfloat16 [2, 8, 1024, 1536], P(None, 'dp', 'seq'), may hold values from -6 to 6
Outputs:
- output: bfloat16 [2, 8, 1024, 1536], P(None, 'dp', 'seq')
- input_grad: float32 [2, 8, 1024, 1536], P(None, 'dp', 'seq')
- grad_query: float32 [1536, 768], P('dp')
- grad_key: float32 [1536, 768], P('dp')
- grad_value: float32 [1536, 768], P('dp')
- grad_mix: float32 [768, 1536], P('dp')
- grad_gate: float32 [1536, 3968], P('dp')
- grad_up: float32 [1536, 3968], P('dp')
- grad_down: float32 [3968, 1536], P('dp')
- grad_attn_gain: float32 [1536], P('dp')
- grad_ffn_gain: float32 [1536], P('dp')
- grad_bias_table: float32 [32, 12], P(None, 'seq')
Inputs may be any that keep to these rules, and one draw needn't show every extreme that they name: bucket_ids[j] is the bucket of the key-minus-query offset j - 1024: offsets 0 to 7 apart have a bucket each, farther offsets share 8 more buckets by distance, the last of them beginning at most 128 apart; positive offsets add half of 32.
All inputs are finite; a program needn't handle non-finite values.
Results may differ from a plain program's by a relative error of at most 0.017.
Values may be sent and summed in bfloat16 or wider, within the bound.
No kernel may reach another device: no remote copies, remote signals or barrier semaphores. Data moves between devices by JAX's collectives and lax.ppermute only.
A program may use at most 320 MiB of HBM per device.

v0:
```python
import jax
import jax.numpy as jnp
from jax import lax
from jax.sharding import PartitionSpec as P

epsilon = 1e-06
gelu_scale = 0.7978845608028654
gelu_cubic = 0.044715


def rms_forward(features):
    inverse = lax.rsqrt(jnp.mean(features * features, axis=-1, keepdims=True) + epsilon)
    return (features * inverse, inverse)


def rms_backward(upstream, normed, inverse, gain):
    scaled = upstream * gain
    return inverse * (scaled - normed * jnp.mean(scaled * normed, axis=-1, keepdims=True))


def gelu_pair(gate_pre):
    inner_argument = gelu_scale * (gate_pre + gelu_cubic * gate_pre * gate_pre * gate_pre)
    tanh_part = jnp.tanh(inner_argument)
    gelu_value = 0.5 * gate_pre * (1.0 + tanh_part)
    gelu_slope = 0.5 * (1.0 + tanh_part) + 0.5 * gate_pre * (
        1.0 - tanh_part * tanh_part
    ) * gelu_scale * (1.0 + 3.0 * gelu_cubic * gate_pre * gate_pre)
    return (gelu_value, gelu_slope)


def project(left_operand, right_operand):
    return jnp.einsum(
        "qoz,zx->qox", left_operand, right_operand, preferred_element_type=jnp.float32
    )


def project_back(left_operand, right_operand):
    return jnp.einsum(
        "kgn,un->kgu", left_operand, right_operand, preferred_element_type=jnp.float32
    )


def outer_sum(left_operand, right_operand):
    return jnp.einsum(
        "ntg,ntq->gq", left_operand, right_operand, preferred_element_type=jnp.float32
    )


def offset_onehot(bucket_ids, bucket_count):
    return (bucket_ids[:, None] == jnp.arange(bucket_count, dtype=jnp.int32)[None, :]).astype(
        jnp.float32
    )


def bias_grid(onehot, table, length):
    two_len = 2 * length
    per_offset = jnp.dot(onehot, table, precision=lax.Precision.HIGHEST)
    shifted = jnp.roll(jnp.transpose(per_offset), -length, axis=1)
    head_count = shifted.shape[0]
    tiled = jnp.tile(shifted, (1, length))
    trimmed = tiled[:, : length * (two_len - 1)].reshape(head_count, length, two_len - 1)
    return trimmed[:, :, :length]


def offset_sums(score_grad, row_start, length):
    head_count, block_rows, unused = score_grad.shape
    two_len = 2 * length
    flipped = jnp.flip(score_grad, axis=1).astype(jnp.float32)
    padded = jnp.pad(flipped, ((0, 0), (0, 0), (0, length)))
    flat = padded.reshape(head_count, block_rows * two_len)[:, : block_rows * (two_len - 1)]
    diagonal = jnp.sum(flat.reshape(head_count, block_rows, two_len - 1), axis=1)[
        :, : block_rows + length - 1
    ]
    start = length - (block_rows - 1) - row_start
    return lax.dynamic_update_slice(
        jnp.zeros((head_count, two_len), jnp.float32), diagonal, (jnp.int32(0), start)
    )


def attend_forward(query_rows, key_rows, value_rows, bias_full, head_count):
    length = query_rows.shape[0]
    block_rows = min(512, length)
    block_count = length // block_rows
    query_blocks = query_rows.reshape(block_count, block_rows, head_count, -1)
    key_heads = key_rows.reshape(length, head_count, -1)
    value_heads = value_rows.reshape(length, head_count, -1)
    starts = jnp.arange(block_count, dtype=jnp.int32) * block_rows

    def one_block(inputs):
        query_block, row_start = inputs
        bias_block = lax.dynamic_slice_in_dim(bias_full, row_start, block_rows, 1)
        scores = (
            jnp.einsum("qhd,khd->hqk", query_block, key_heads, preferred_element_type=jnp.float32)
            + bias_block
        )
        row_max = jnp.max(scores, axis=-1, keepdims=True)
        expo = jnp.exp(scores - row_max)
        row_total = jnp.sum(expo, axis=-1, keepdims=True)
        probs_low = (expo / row_total).astype(jnp.bfloat16)
        attended = jnp.einsum(
            "hqk,khd->qhd", probs_low, value_heads, preferred_element_type=jnp.float32
        )
        return (
            attended.reshape(block_rows, -1).astype(jnp.bfloat16),
            (row_max + jnp.log(row_total))[:, :, 0],
        )

    attended, log_sums = lax.map(one_block, (query_blocks, starts))
    return (attended.reshape(length, -1), log_sums)


def attend_backward(
    query_rows, key_rows, value_rows, grad_rows, log_sums, bias_full, offset_total, head_count
):
    length = query_rows.shape[0]
    block_rows = min(512, length)
    block_count = length // block_rows
    query_blocks = query_rows.reshape(block_count, block_rows, head_count, -1)
    grad_blocks = grad_rows.reshape(block_count, block_rows, head_count, -1)
    key_heads = key_rows.reshape(length, head_count, -1)
    value_heads = value_rows.reshape(length, head_count, -1)
    starts = jnp.arange(block_count, dtype=jnp.int32) * block_rows

    def one_block(running, inputs):
        key_grad, value_grad, offset_run = running
        query_block, grad_block, log_block, row_start = inputs
        bias_block = lax.dynamic_slice_in_dim(bias_full, row_start, block_rows, 1)
        scores = (
            jnp.einsum("qhd,khd->hqk", query_block, key_heads, preferred_element_type=jnp.float32)
            + bias_block
        )
        attn_probs = jnp.exp(scores - log_block[:, :, None])
        prob_grad = jnp.einsum(
            "qhd,khd->hqk", grad_block, value_heads, preferred_element_type=jnp.float32
        )
        centred = jnp.sum(attn_probs * prob_grad, axis=-1, keepdims=True)
        score_grad = (attn_probs * (prob_grad - centred)).astype(jnp.bfloat16)
        query_grad = jnp.einsum(
            "hqk,khd->qhd", score_grad, key_heads, preferred_element_type=jnp.float32
        )
        key_grad = key_grad + jnp.einsum(
            "hqk,qhd->khd", score_grad, query_block, preferred_element_type=jnp.float32
        )
        value_grad = value_grad + jnp.einsum(
            "hqk,qhd->khd",
            attn_probs.astype(jnp.bfloat16),
            grad_block,
            preferred_element_type=jnp.float32,
        )
        offset_run = offset_run + offset_sums(score_grad, row_start, length)
        return (
            (key_grad, value_grad, offset_run),
            query_grad.reshape(block_rows, -1).astype(jnp.bfloat16),
        )

    start_state = (
        jnp.zeros(key_heads.shape, jnp.float32),
        jnp.zeros(value_heads.shape, jnp.float32),
        offset_total,
    )
    final_state, query_grad = lax.scan(
        one_block, start_state, (query_blocks, grad_blocks, log_sums, starts)
    )
    key_grad, value_grad, offset_total = final_state
    return (
        query_grad.reshape(length, -1),
        key_grad.reshape(length, -1).astype(jnp.bfloat16),
        value_grad.reshape(length, -1).astype(jnp.bfloat16),
        offset_total,
    )


def reduce_grads(grad_set):
    g_query, g_key, g_value, g_mix, g_gate, g_up, g_down, g_attn, g_ffn = grad_set
    owner_part = (
        lax.psum_scatter(g_query, "dp", scatter_dimension=0, tiled=True),
        lax.psum_scatter(g_key, "dp", scatter_dimension=0, tiled=True),
        lax.psum_scatter(g_value, "dp", scatter_dimension=0, tiled=True),
        lax.psum_scatter(g_mix, "dp", scatter_dimension=0, tiled=True),
        lax.psum_scatter(g_gate, "dp", scatter_dimension=0, tiled=True),
        lax.psum_scatter(g_up, "dp", scatter_dimension=0, tiled=True),
        lax.psum_scatter(g_down, "dp", scatter_dimension=0, tiled=True),
        lax.psum_scatter(g_attn, "dp", scatter_dimension=0, tiled=True),
        lax.psum_scatter(g_ffn, "dp", scatter_dimension=0, tiled=True),
    )
    o_query, o_key, o_value, o_mix, o_gate, o_up, o_down, o_attn, o_ffn = owner_part
    return (
        lax.psum(o_query.astype(jnp.bfloat16), "seq").astype(jnp.float32),
        lax.psum(o_key.astype(jnp.bfloat16), "seq").astype(jnp.float32),
        lax.psum(o_value.astype(jnp.bfloat16), "seq").astype(jnp.float32),
        lax.psum(o_mix.astype(jnp.bfloat16), "seq").astype(jnp.float32),
        lax.psum(o_gate.astype(jnp.bfloat16), "seq").astype(jnp.float32),
        lax.psum(o_up.astype(jnp.bfloat16), "seq").astype(jnp.float32),
        lax.psum(o_down.astype(jnp.bfloat16), "seq").astype(jnp.float32),
        lax.psum(o_attn.astype(jnp.bfloat16), "seq").astype(jnp.float32),
        lax.psum(o_ffn.astype(jnp.bfloat16), "seq").astype(jnp.float32),
    )


def per_device(
    tokens,
    query_weight,
    key_weight,
    value_weight,
    mix_weight,
    gate_weight,
    up_weight,
    down_weight,
    attn_gain,
    ffn_gain,
    bias_table,
    bucket_ids,
    out_grad,
):
    micro_count = tokens.shape[0]
    head_local = bias_table.shape[1]
    bucket_count = bias_table.shape[0]
    length = bucket_ids.shape[0] // 2
    onehot = offset_onehot(bucket_ids, bucket_count)
    bias_full = bias_grid(onehot, bias_table, length)
    offset_total = jnp.zeros((head_local, 2 * length), jnp.float32)
    outputs_list = []
    input_grads = []
    running = None
    for micro_index in range(micro_count):
        gathered = (
            lax.all_gather(query_weight, "dp", axis=0, tiled=True),
            lax.all_gather(key_weight, "dp", axis=0, tiled=True),
            lax.all_gather(value_weight, "dp", axis=0, tiled=True),
            lax.all_gather(mix_weight, "dp", axis=0, tiled=True),
            lax.all_gather(gate_weight, "dp", axis=0, tiled=True),
            lax.all_gather(up_weight, "dp", axis=0, tiled=True),
            lax.all_gather(down_weight, "dp", axis=0, tiled=True),
            lax.all_gather(attn_gain, "dp", axis=0, tiled=True),
            lax.all_gather(ffn_gain, "dp", axis=0, tiled=True),
        )
        (
            full_query,
            full_key,
            full_value,
            full_mix,
            full_gate,
            full_up,
            full_down,
            full_attn,
            full_ffn,
        ) = gathered
        gain_one = full_attn.astype(jnp.float32)
        gain_two = full_ffn.astype(jnp.float32)
        inputs = tokens[micro_index].astype(jnp.float32)
        normed_attn, inverse_attn = rms_forward(inputs)
        normed_low = (normed_attn * gain_one).astype(jnp.bfloat16)
        query_tok = project(normed_low, full_query).astype(jnp.bfloat16)
        key_tok = project(normed_low, full_key).astype(jnp.bfloat16)
        value_tok = project(normed_low, full_value).astype(jnp.bfloat16)
        query_seq, key_seq, value_seq = (
            lax.all_to_all(query_tok, "seq", split_axis=2, concat_axis=1, tiled=True),
            lax.all_to_all(key_tok, "seq", split_axis=2, concat_axis=1, tiled=True),
            lax.all_to_all(value_tok, "seq", split_axis=2, concat_axis=1, tiled=True),
        )
        sequence_index = 0
        attended_one, log_one = attend_forward(
            query_seq[sequence_index],
            key_seq[sequence_index],
            value_seq[sequence_index],
            bias_full,
            head_local,
        )
        attended_list = [attended_one]
        log_list = [log_one]
        attended_seq = jnp.stack(attended_list)
        attended_tok = lax.all_to_all(attended_seq, "seq", split_axis=1, concat_axis=2, tiled=True)
        middle = inputs + project(attended_tok, full_mix)
        normalized_feedforward, inverse_ffn = rms_forward(middle)
        ffn_low = (normalized_feedforward * gain_two).astype(jnp.bfloat16)
        gate_pre = project(ffn_low, full_gate)
        up_pre = project(ffn_low, full_up)
        gelu_value, gelu_slope = gelu_pair(gate_pre)
        hidden = (gelu_value * up_pre).astype(jnp.bfloat16)
        result = middle + project(hidden, full_down)
        outputs_list.append(result.astype(jnp.bfloat16))
        regathered = (
            lax.all_gather(query_weight, "dp", axis=0, tiled=True),
            lax.all_gather(key_weight, "dp", axis=0, tiled=True),
            lax.all_gather(value_weight, "dp", axis=0, tiled=True),
            lax.all_gather(mix_weight, "dp", axis=0, tiled=True),
            lax.all_gather(gate_weight, "dp", axis=0, tiled=True),
            lax.all_gather(up_weight, "dp", axis=0, tiled=True),
            lax.all_gather(down_weight, "dp", axis=0, tiled=True),
            lax.all_gather(attn_gain, "dp", axis=0, tiled=True),
            lax.all_gather(ffn_gain, "dp", axis=0, tiled=True),
        )
        (
            full_query,
            full_key,
            full_value,
            full_mix,
            full_gate,
            full_up,
            full_down,
            full_attn,
            full_ffn,
        ) = regathered
        gain_one = full_attn.astype(jnp.float32)
        gain_two = full_ffn.astype(jnp.float32)
        cotangent = out_grad[micro_index]
        hidden_grad = project_back(cotangent, full_down)
        gate_grad = (hidden_grad * up_pre * gelu_slope).astype(jnp.bfloat16)
        up_grad = (hidden_grad * gelu_value).astype(jnp.bfloat16)
        ffn_in_grad = project_back(gate_grad, full_gate) + project_back(up_grad, full_up)
        middle_grad = cotangent.astype(jnp.float32) + rms_backward(
            ffn_in_grad, normalized_feedforward, inverse_ffn, gain_two
        )
        mix_in = middle_grad.astype(jnp.bfloat16)
        attended_grad = project_back(mix_in, full_mix).astype(jnp.bfloat16)
        grad_seq = lax.all_to_all(attended_grad, "seq", split_axis=2, concat_axis=1, tiled=True)
        sequence_index = 0
        query_one, key_one, value_one, offset_total = attend_backward(
            query_seq[sequence_index],
            key_seq[sequence_index],
            value_seq[sequence_index],
            grad_seq[sequence_index],
            log_list[sequence_index],
            bias_full,
            offset_total,
            head_local,
        )
        query_list = [query_one]
        key_list = [key_one]
        value_list = [value_one]
        query_gs = jnp.stack(query_list)
        key_gs = jnp.stack(key_list)
        value_gathered_rows = jnp.stack(value_list)
        query_gt, key_gt, value_gt = (
            lax.all_to_all(query_gs, "seq", split_axis=1, concat_axis=2, tiled=True),
            lax.all_to_all(key_gs, "seq", split_axis=1, concat_axis=2, tiled=True),
            lax.all_to_all(value_gathered_rows, "seq", split_axis=1, concat_axis=2, tiled=True),
        )
        attn_in_grad = (
            project_back(query_gt, full_query)
            + project_back(key_gt, full_key)
            + project_back(value_gt, full_value)
        )
        input_grads.append(
            middle_grad + rms_backward(attn_in_grad, normed_attn, inverse_attn, gain_one)
        )
        grad_set = (
            outer_sum(normed_low, query_gt),
            outer_sum(normed_low, key_gt),
            outer_sum(normed_low, value_gt),
            outer_sum(attended_tok, mix_in),
            outer_sum(ffn_low, gate_grad),
            outer_sum(ffn_low, up_grad),
            outer_sum(hidden, cotangent),
            jnp.sum(attn_in_grad * normed_attn, axis=(0, 1)),
            jnp.sum(ffn_in_grad * normalized_feedforward, axis=(0, 1)),
        )
        running = grad_set if running is None else jax.tree.map(jnp.add, running, grad_set)
    running = reduce_grads(running)
    (
        grad_query,
        grad_key,
        grad_value,
        grad_mix,
        grad_gate,
        grad_up,
        grad_down,
        grad_attn_gain,
        grad_ffn_gain,
    ) = running
    table_local = jnp.transpose(jnp.dot(offset_total, onehot, precision=lax.Precision.HIGHEST))
    grad_bias_table = lax.psum(table_local, "dp")
    output = jnp.stack(outputs_list)
    input_grad = jnp.stack(input_grads)
    return (
        output,
        input_grad,
        grad_query,
        grad_key,
        grad_value,
        grad_mix,
        grad_gate,
        grad_up,
        grad_down,
        grad_attn_gain,
        grad_ffn_gain,
        grad_bias_table,
    )


def solution(mesh):
    in_specs = (
        P(None, "dp", "seq", None),
        P("dp", None),
        P("dp", None),
        P("dp", None),
        P("dp", None),
        P("dp", None),
        P("dp", None),
        P("dp", None),
        P("dp"),
        P("dp"),
        P(None, "seq"),
        P(),
        P(None, "dp", "seq", None),
    )
    out_specs = (
        P(None, "dp", "seq", None),
        P(None, "dp", "seq", None),
        P("dp", None),
        P("dp", None),
        P("dp", None),
        P("dp", None),
        P("dp", None),
        P("dp", None),
        P("dp", None),
        P("dp"),
        P("dp"),
        P(None, "seq"),
    )
    return jax.shard_map(
        per_device, mesh=mesh, in_specs=in_specs, out_specs=out_specs, check_vma=False
    )
```

profile of v0, /device:TPU:0, one launch (start us, length us, event | category | flops | bytes accessed | tf_op | source)
XLA Modules:
  0.0 3240.4 jit_solution(11964022169080834986)
XLA Ops:
  24.5 33.4 %copy.199 = f32[1,3,1024,2048]{3,1,2,0:T(4,128)} copy(f32[1,3,1024,2048]{3,2,1,0:T(8,128)} %broadcast_bitcast_fusion) | data formatting | bytes 50331648
  57.9 22.9 slice_bitcast_fusion
  82.7 24.6 all-reduce.7
  107.3 466.3 %while.67 = (u32[]{:T(128)}, f32[1,3,2096128]{2,1,0:T(4,128)}, f32[6288384]{0:T(1024)}, u32[]{}, f32[]{:T(128)}, /*index=5*/u32[]{}, u32[]{}, u32[]{}) while((u32[]{:T(128)}, f32[1,3,2096128]{2,1,0:T(4,128)}, f32[6288384]{0:T(1024)}, u32[]{}, f32[]{:T(128)}, /*index=5*/u32[]{}, u32[]{}, u32[]{}) %tuple.145), condition=%wide.cond, body=%wide.body.sunk | while | flops 9 | bytes 33538248
  107.8 83.8 %dynamic-slice_reduce_fusion.2 = f32[2096128]{0:T(1024)} fusion(f32[]{:T(128)} %broadcast.402, f32[1,3,2096128]{2,1,0:T(4,128)} %get-tuple-element.1099, u32[]{:T(128)S(6)} %multiply.66, u32[]{:T(128)S(6)} %multiply.67), kind=kLoop, calls=%fused_computation.230.clone.1 | loop fusion | bytes 16769036
  191.6 71.1 %dynamic-update-slice.12 = f32[6288384]{0:T(1024)} dynamic-update-slice(f32[6288384]{0:T(1024)} %get-tuple-element.1092, f32[2096128]{0:T(1024)} %dynamic-slice_reduce_fusion.2, u32[]{:T(128)S(6)} %add.553) | dynamic-update-slice | bytes 16769028
  263.3 83.8 %dynamic-slice_reduce_fusion.2 = f32[2096128]{0:T(1024)} fusion(f32[]{:T(128)} %broadcast.402, f32[1,3,2096128]{2,1,0:T(4,128)} %get-tuple-element.1099, u32[]{:T(128)S(6)} %multiply.66, u32[]{:T(128)S(6)} %multiply.67), kind=kLoop, calls=%fused_computation.230.clone.1 | loop fusion | bytes 16769036
  347.0 71.2 %dynamic-update-slice.12 = f32[6288384]{0:T(1024)} dynamic-update-slice(f32[6288384]{0:T(1024)} %get-tuple-element.1092, f32[2096128]{0:T(1024)} %dynamic-slice_reduce_fusion.2, u32[]{:T(128)S(6)} %add.553) | dynamic-update-slice | bytes 16769028
  418.7 83.7 %dynamic-slice_reduce_fusion.2 = f32[2096128]{0:T(1024)} fusion(f32[]{:T(128)} %broadcast.402, f32[1,3,2096128]{2,1,0:T(4,128)} %get-tuple-element.1099, u32[]{:T(128)S(6)} %multiply.66, u32[]{:T(128)S(6)} %multiply.67), kind=kLoop, calls=%fused_computation.230.clone.1 | loop fusion | bytes 16769036
  502.4 71.2 %dynamic-update-slice.12 = f32[6288384]{0:T(1024)} dynamic-update-slice(f32[6288384]{0:T(1024)} %get-tuple-element.1092, f32[2096128]{0:T(1024)} %dynamic-slice_reduce_fusion.2, u32[]{:T(128)S(6)} %add.553) | dynamic-update-slice | bytes 16769028
  573.6 38.0 %reshape.809 = f32[3,1024,2047]{2,1,0:T(8,128)} reshape(f32[6288384]{0:T(1024)} %get-tuple-element.658) | data formatting | bytes 50307072 | tf_op jit(solution)/shard_map/reshape | solution.py:61
  705.6 22.7 while.64
  747.6 22.7 while.63
  952.1 316.5 %while.65 = (s32[]{:T(128)}, f32[1024,3,64]{0,2,1:T(8,128)}, f32[1024,3,64]{0,2,1:T(8,128)}, f32[3,2048]{1,0:T(4,128)}, bf16[2,512,192]{1,2,0:T(8,128)(2,1)}, /*...) while((s32[]{:T(128)}, f32[1024,3,64]{0,2,1:T(8,128)}, ...), condition=%wide.region_16.17_spmd.clone, body=%wide.region_13.16_spmd.clone.sunk | while | flops 1026385920 | bytes 241739168 | solution.py:161
  997.6 30.6 rev.17
  1054.6 35.3 %reshape.893 = f32[3144192]{0:T(1024)} reshape(f32[3,1048064]{1,0:T(4,128)} %slice_convert_fusion.4) | data formatting | bytes 25153536 | tf_op jit(solution)/shard_map/while
  1089.9 19.3 reshape.894
  1144.9 30.6 rev.17
  1201.9 35.3 %reshape.893 = f32[3144192]{0:T(1024)} reshape(f32[3,1048064]{1,0:T(4,128)} %slice_convert_fusion.4) | data formatting | bytes 25153536 | tf_op jit(solution)/shard_map/while
  1237.2 19.3 reshape.894
  1272.9 321.2 %while.66 = (s32[]{:T(128)}, f32[1024,3,64]{0,2,1:T(8,128)}, f32[1024,3,64]{0,2,1:T(8,128)}, f32[3,2048]{1,0:T(4,128)}, bf16[2,512,192]{1,2,0:T(8,128)(2,1)}, /*...) while((s32[]{:T(128)}, f32[1024,3,64]{0,2,1:T(8,128)}, ...), condition=%wide.region_22.23_spmd.clone, body=%wide.region_19.22_spmd.clone.sunk | while | flops 1026385920 | bytes 241739168 | solution.py:161
  1317.8 30.6 rev.18
  1374.5 35.0 %reshape.896 = f32[3144192]{0:T(1024)} reshape(f32[3,1048064]{1,0:T(4,128)} %slice_convert_fusion.5) | data formatting | bytes 25153536 | tf_op jit(solution)/shard_map/while
  1464.4 30.6 rev.18
  1521.2 35.0 %reshape.896 = f32[3144192]{0:T(1024)} reshape(f32[3,1048064]{1,0:T(4,128)} %slice_convert_fusion.5) | data formatting | bytes 25153536 | tf_op jit(solution)/shard_map/while
  1556.2 19.2 reshape.897
  1833.2 86.8 %reduce-scatter.12.cloned.1.call-done = f32[192,768]{1,0:T(8,128)} async-done(((f32[1536,768]{1,0:T(8,128)}), f32[192,768]{1,0:T(8,128)}) %reduce-scatter.12.cloned.1.call-update) | async-done | bytes 589840 | tf_op jit(solution)/shard_map/reduce_scatter | solution.py:178
  1921.8 394.1 %reduce-scatter.16.cloned.1.call-done = f32[192,3968]{1,0:T(8,128)} async-done(((f32[1536,3968]{1,0:T(8,128)}), f32[192,3968]{1,0:T(8,128)}) %reduce-scatter.16.cloned.1.call-update) | async-done | bytes 3047440 | tf_op jit(solution)/shard_map/reduce_scatter | solution.py:180
  2319.0 392.2 %reduce-scatter.18.cloned.1.call-done = f32[192,3968]{1,0:T(8,128)} async-done(((f32[1536,3968]{1,0:T(8,128)}), f32[192,3968]{1,0:T(8,128)}) %reduce-scatter.18.cloned.1.call-update) | async-done | bytes 3047440 | tf_op jit(solution)/shard_map/reduce_scatter | solution.py:181
  2714.5 392.0 %reduce-scatter.20.cloned.1.call-done = f32[496,1536]{1,0:T(8,128)} async-done(((f32[3968,1536]{1,0:T(8,128)}), f32[496,1536]{1,0:T(8,128)}) %reduce-scatter.20.cloned.1.call-update) | async-done | bytes 3047440 | tf_op jit(solution)/shard_map/reduce_scatter | solution.py:182
  3120.0 35.7 %all-reduce.6 = (bf16[1536]{0:T(1024)(128)(2,1)S(1)}, bf16[1536]{0:T(1024)(128)(2,1)S(1)}, f32[32,3]{0,1:T(4,128)}) all-reduce(f32[1536]{0:T(1024)S(1)} %add.358, f32[1536]{0:T(1024)} %add.359, f32[32,3]{0,1:T(4,128)} %fusion.112), channel_id=9, replica_groups=mesh['dp'=8,'seq'=4] {'dp'}, use_global_device_ids=true, to_apply=%region_40.41.clone | all-reduce | flops 3168 | bytes 19200
  3170.0 51.2 %all-reduce.12.cloned.1.call-done = (bf16[192,768]{1,0:T(8,128)(2,1)}, bf16[192,768]{1,0:T(8,128)(2,1)}, bf16[192,768]{1,0:T(8,128)(2,1)}, bf16[96,1536]{1,0:T(8...) async-done(((bf16[192,768]{1,0:T(8,128)(2,1)}, bf16[192,768]{1,0:T(8,128)(2,1)}, bf16[192,768]{1,0:T(8,128)(2,1)}, ...) | async-done | bytes 5750800 | tf_op jit(solution)/shard_map/psum | solution.py:188
  (597 shorter events, 895.7 us)
Async XLA Ops:
  7.2 617.0 %all-gather.8.cloned.1.call-start = ((), (), s32[]{:S(2)}) async-start(), calls=%async_computation.23 | async-start | bytes 2654208 | tf_op jit(solution)/shard_map/all_gather | solution.py:227
  7.9 627.4 %all-gather.10.cloned.1.call-start = ((), (), s32[]{:S(2)}) async-start(), calls=%async_computation.24 | async-start | bytes 2654208 | tf_op jit(solution)/shard_map/all_gather | solution.py:228
  8.7 638.4 %all-gather.12.cloned.1.call-start = ((), (), s32[]{:S(2)}) async-start(), calls=%async_computation.25 | async-start | bytes 2654208 | tf_op jit(solution)/shard_map/all_gather | solution.py:229
  9.4 790.2 %all-gather.14.cloned.1.call-start = ((), (), s32[]{:S(2)}) async-start(), calls=%async_computation.26 | async-start | bytes 2654208 | tf_op jit(solution)/shard_map/all_gather | solution.py:230
  10.0 794.6 %all-gather.16.cloned.1.call-start = ((), (), s32[]{:S(2)}) async-start(), calls=%async_computation.27 | async-start | bytes 13713408 | tf_op jit(solution)/shard_map/all_gather | solution.py:231
  10.6 803.9 %all-gather.18.cloned.1.call-start = ((), (), s32[]{:S(2)}) async-start(), calls=%async_computation.28 | async-start | bytes 13713408 | tf_op jit(solution)/shard_map/all_gather | solution.py:232
  11.2 813.1 %all-gather.20.cloned.1.call-start = ((), (), s32[]{:S(2)}) async-start(), calls=%async_computation.29 | async-start | bytes 13713408 | tf_op jit(solution)/shard_map/all_gather | solution.py:233
  107.3 577.4 %copy-start.53 = (f32[1536]{0:T(1024)}, f32[1536]{0:T(1024)S(1)}, u32[]{:S(2)}) copy-start(f32[1536]{0:T(1024)S(1)} %convert_element_type.443) | copy-start | bytes 18436
  631.8 11.3 all-to-all-start.4
  643.1 13.4 all-to-all-start.5
  656.5 12.9 all-to-all-start.6
  670.1 10.9 all-to-all-start
  681.0 19.6 all-to-all-start.1
  700.6 38.4 %all-to-all-start.2 = ((bf16[4,2,24576]{2,1,0:T(2,128)(2,1)}), bf16[4,2,24576]{2,1,0:T(2,128)(2,1)}, u32[]{:S(2)}, u32[]{:S(2)}) async-start(bf16[4,2,24576]{2,1,0:T(2,128)(2,1)} %reshape.866), calls=%async_computation.2 | async-start | bytes 786432 | tf_op jit(solution)/shard_map/all_to_all | solution.py:259
  739.0 43.1 %all-to-all-start.7 = ((bf16[4,2,24576]{2,1,0:T(2,128)(2,1)}), bf16[4,2,24576]{2,1,0:T(2,128)(2,1)}, u32[]{:S(2)}, u32[]{:S(2)}) async-start(bf16[4,2,24576]{2,1,0:T(2,128)(2,1)} %reshape.860), calls=%async_computation.7 | async-start | bytes 786432 | tf_op jit(solution)/shard_map/all_to_all | solution.py:272
  782.1 12.1 all-to-all-start.3
  926.7 16.3 all-to-all-start.8
  930.8 896.9 %reduce-scatter.14.cloned.1.call-start = ((), (), s32[]{:S(2)}) async-start(), calls=%async_computation.33 | async-start | bytes 5308416 | tf_op jit(solution)/shard_map/reduce_scatter | solution.py:179
  943.0 325.6 %all-to-all-start.12 = ((bf16[4,2,24576]{2,1,0:T(2,128)(2,1)}), bf16[4,2,24576]{2,1,0:T(2,128)(2,1)}, u32[]{:S(2)}, u32[]{:S(2)}) async-start(bf16[4,2,24576]{2,1,0:T(2,128)(2,1)} %reshape.872), calls=%async_computation.12 | async-start | bytes 786432 | tf_op jit(solution)/shard_map/all_to_all | solution.py:316
  1601.2 10.9 all-to-all-start.13
  1612.1 10.9 all-to-all-start.9
  1615.6 214.0 %reduce-scatter.8.cloned.1.call-start = ((), (), s32[]{:S(2)}) async-start(), calls=%async_computation.30 | async-start | bytes 5308416 | tf_op jit(solution)/shard_map/reduce_scatter | solution.py:176
  1642.7 10.9 all-to-all-start.14
  1653.6 12.0 all-to-all-start.10
  1658.1 173.2 %reduce-scatter.10.cloned.1.call-start = ((), (), s32[]{:S(2)}) async-start(), calls=%async_computation.31 | async-start | bytes 5308416 | tf_op jit(solution)/shard_map/reduce_scatter | solution.py:177
  1686.9 11.0 all-to-all-start.15
  1698.0 11.6 all-to-all-start.11
  1702.1 217.9 %reduce-scatter.12.cloned.1.call-start = ((), (), s32[]{:S(2)}) async-start(), calls=%async_computation.32 | async-start | bytes 5308416 | tf_op jit(solution)/shard_map/reduce_scatter | solution.py:178
  1717.2 598.7 %reduce-scatter.16.cloned.1.call-start = ((), (), s32[]{:S(2)}) async-start(), calls=%async_computation.34 | async-start | bytes 27426816 | tf_op jit(solution)/shard_map/reduce_scatter | solution.py:180
  1746.6 964.6 %reduce-scatter.18.cloned.1.call-start = ((), (), s32[]{:S(2)}) async-start(), calls=%async_computation.35 | async-start | bytes 27426816 | tf_op jit(solution)/shard_map/reduce_scatter | solution.py:181
  1775.4 1331.0 %reduce-scatter.20.cloned.1.call-start = ((), (), s32[]{:S(2)}) async-start(), calls=%async_computation.36 | async-start | bytes 27426816 | tf_op jit(solution)/shard_map/reduce_scatter | solution.py:182
  1805.0 1416.2 %all-reduce.12.cloned.1.call-start = ((), (), s32[]{:S(2)}) async-start(), calls=%async_computation.37 | async-start | bytes 11501568 | tf_op jit(solution)/shard_map/psum | solution.py:188
  (102 other events, 686.5 us)
Sparse Core Ops, SparseCore 0:
  10.2 54.7 all-gather.7
  67.2 51.0 all-gather.9
  120.5 50.8 all-gather.11
  173.4 50.6 all-gather.13
  226.1 170.2 all-gather.15
  398.4 169.8 all-gather.17
  570.5 169.8 all-gather.19
  943.1 93.1 reduce-scatter.13
  1631.1 91.3 reduce-scatter.7
  1726.0 95.1 reduce-scatter.9
  1824.8 95.1 reduce-scatter.11
  1923.8 392.0 reduce-scatter.15
  2319.8 391.3 reduce-scatter.17
  2715.0 391.3 reduce-scatter.19
  3109.8 111.2 all-reduce.11
where the time goes:
time: 3270 us; the launch traced here: 3240 us
  waiting for transfers between devices  1350 us (41%)
  local copies, waits for them, and re-layouts  1130 us (35%)
  matrix products  368 us (11%)
  other arithmetic  182 us (6%)
  loops' own time  70.7 us (2%)
  blocking collectives  66.8 us (2%)
  starting transfers between devices  63.2 us (2%)
    unnamed x220, local copies, waits for them, and re-layouts  594 us
    reduce_scatter x1, waiting for transfers between devices, reduce_grads(): lax.psum_scatter(g_gate, 'dp', scatter_dimension=0, tiled=True)  394 us
    reduce_scatter x1, waiting for transfers between devices, reduce_grads(): lax.psum_scatter(g_up, 'dp', scatter_dimension=0, tiled=True)  392 us
    reduce_scatter x1, waiting for transfers between devices, reduce_grads(): lax.psum_scatter(g_down, 'dp', scatter_dimension=0, tiled=True)  392 us
    while x60, local copies, waits for them, and re-layouts  221 us
    rev x4, local copies, waits for them, and re-layouts, offset_sums(): flipped = jnp.flip(score_grad, axis=1).astype(jnp.float32)  122 us
    dot_general x14, matrix products, outer_sum(): jnp.einsum('ntg,ntq->gq', left_operand, right_operand, preferred_element_...  105 us
    reduce_scatter x1, waiting for transfers between devices, reduce_grads(): lax.psum_scatter(g_value, 'dp', scatter_dimension=0, tiled=True)  86.8 us
  transfers between devices with their start and end apart: 31, of which 13 were waited for; matrix products, arithmetic and copies ran while one was open for 47% of the time, Pallas kernels for 0%

commit v1 on v0

v1 whole, which is shorter than its diff:
```python
import functools

import jax
import jax.numpy as jnp
from jax import lax
from jax.experimental import pallas as pl
from jax.experimental.pallas import tpu as pltpu
from jax.sharding import PartitionSpec as P

epsilon = 1e-06
gelu_scale = 0.7978845608028654
gelu_cubic = 0.044715
low = jnp.bfloat16
wide = jnp.float32
lanes = 128


def rms_forward(features):
    inverse = lax.rsqrt(jnp.mean(features * features, axis=-1, keepdims=True) + epsilon)
    return (features * inverse, inverse)


def rms_backward(upstream, normed, inverse, gain):
    scaled = upstream * gain
    return inverse * (scaled - normed * jnp.mean(scaled * normed, axis=-1, keepdims=True))


def gelu_pair(gate_pre):
    inner_argument = gelu_scale * (gate_pre + gelu_cubic * gate_pre * gate_pre * gate_pre)
    tanh_part = jnp.tanh(inner_argument)
    gelu_value = 0.5 * gate_pre * (1.0 + tanh_part)
    gelu_slope = 0.5 * (1.0 + tanh_part) + 0.5 * gate_pre * (
        1.0 - tanh_part * tanh_part
    ) * gelu_scale * (1.0 + 3.0 * gelu_cubic * gate_pre * gate_pre)
    return (gelu_value, gelu_slope)


def mm(left, right, dims, out=low):
    return lax.dot_general(left, right, ((dims[:1], dims[1:]), ((), ())), preferred_element_type=wide).astype(out)


def flip_core(array):
    return lax.ppermute(array, "seq", [(0, 1), (1, 0), (2, 3), (3, 2)])


def flip_y(array):
    return lax.ppermute(array, "seq", [(0, 2), (2, 0), (1, 3), (3, 1)])


def flip_x(array):
    return lax.ppermute(array, "dp", [(d, d ^ 1) for d in range(8)])


def z_up(array, sources):
    return lax.ppermute(array, "dp", [(2 * z + x, 2 * z + 2 + x) for z in sources for x in (0, 1)])


def z_down(array, sources):
    return lax.ppermute(array, "dp", [(2 * z + x, 2 * z - 2 + x) for z in sources for x in (0, 1)])


def gather_dp(shard):
    if lax.axis_size("dp") != 8:
        return lax.all_gather(shard, "dp", axis=0, tiled=False)
    d = lax.axis_index("dp")
    z, x = d // 2, d % 2
    up1, down1, side0 = z_up(shard, (0, 1, 2)), z_down(shard, (1, 2, 3)), flip_x(shard)
    up2, down2 = z_up(up1, (1, 2)), z_down(down1, (2, 1))
    first = jnp.where(z == 0, down1, up1)
    side1 = flip_x(first)
    up3, down3 = z_up(up2, (2,)), z_down(down2, (1,))
    second = jnp.where(z == 0, down2, jnp.where(z == 3, up2, down1))
    side2 = flip_x(second)
    third = jnp.where(z == 0, down3, jnp.where(z == 1, down2, jnp.where(z == 2, up2, up3)))
    side3 = flip_x(third)
    at1 = jnp.where(z == 0, 1, z - 1)
    at2 = jnp.where(z == 0, 2, jnp.where(z == 3, 1, z + 1))
    at3 = jnp.where((z == 0) | (z == 1), 3, 0)
    whole = jnp.zeros((8,) + shard.shape, shard.dtype)
    for block, at, across in (
        (shard, z, x),
        (side0, z, 1 - x),
        (first, at1, x),
        (side1, at1, 1 - x),
        (second, at2, x),
        (side2, at2, 1 - x),
        (third, at3, x),
        (side3, at3, 1 - x),
    ):
        whole = lax.dynamic_update_slice(whole, block[None], (2 * at + across, 0, 0))
    return whole


def scatter_dp(parts):
    if lax.axis_size("dp") != 8:
        return lax.psum_scatter(parts, "dp", scatter_dimension=0, tiled=False)
    d = lax.axis_index("dp")
    z, x = d // 2, d % 2
    by_x = parts.reshape((4, 2) + parts.shape[1:])
    mine = lax.dynamic_index_in_dim(by_x, x, 1, keepdims=False)
    other = lax.dynamic_index_in_dim(by_x, 1 - x, 1, keepdims=False)
    mine = (mine.astype(wide) + flip_x(other).astype(wide)).astype(low)

    def block(index):
        return lax.dynamic_index_in_dim(mine, jnp.clip(index, 0, 3), 0, keepdims=False)

    def joined(left, right):
        return (left.astype(wide) + right.astype(wide)).astype(low)

    up, down = z_up(block(z + 3), (0,)), z_down(block(z - 3), (3,))
    up, down = z_up(joined(block(z + 2), up), (0, 1)), z_down(joined(block(z - 2), down), (3, 2))
    up, down = z_up(joined(block(z + 1), up), (0, 1, 2)), z_down(joined(block(z - 1), down), (3, 2, 1))
    return block(z).astype(wide) + up.astype(wide) + down.astype(wide)


def sum_dp(small):
    size = lax.axis_size("dp")
    step = 1
    while step < size:
        small = small + lax.ppermute(small, "dp", [(d, d ^ step) for d in range(size)])
        step *= 2
    return small


def gather_seq(block):
    pair = jnp.stack([block, flip_y(block)])
    return jnp.concatenate([pair, flip_core(pair)])


def scatter_seq(parts):
    back = flip_core(parts[2:4])
    away = (parts[1].astype(wide) + back[1].astype(wide)).astype(low)
    return parts[0].astype(wide) + back[0].astype(wide) + flip_y(away).astype(wide)


def by_slot(groups, s):
    grid = groups.reshape((2, 2) + groups.shape[1:])
    grid = jnp.swapaxes(grid, 0, 1)
    grid = jnp.where(s % 2 == 1, grid[::-1], grid)
    grid = jnp.where(s // 2 == 1, grid[:, ::-1], grid)
    return grid.reshape(groups.shape)


def by_index(slots, s):
    grid = slots.reshape((2, 2) + slots.shape[1:])
    grid = jnp.where(s % 2 == 1, grid[::-1], grid)
    grid = jnp.where(s // 2 == 1, grid[:, ::-1], grid)
    return jnp.swapaxes(grid, 0, 1).reshape(slots.shape)


def quarter_of(per):
    return -(-(-(-per // 4)) // 16) * 16


def pick_kernel(s_ref, gate_ref, up_ref, out_ref, *, owners, per, quarter):
    for choice in range(4):

        @pl.when(s_ref[0] == choice)
        def _():
            width = min(quarter, per - choice * quarter)
            for half, ref in enumerate((gate_ref, up_ref)):
                for d in range(owners):
                    start = d * per + choice * quarter
                    piece = ref[:, start : start + width]
                    if width < quarter:
                        piece = jnp.concatenate(
                            [piece, jnp.zeros((piece.shape[0], quarter - width), piece.dtype)], axis=1
                        )
                    to = (half * owners + d) * quarter
                    out_ref[:, to : to + quarter] = piece


def pick_columns(gate, up, s):
    owners = lax.axis_size("dp")
    rows, total = gate.shape
    per = total // owners
    quarter = quarter_of(per)
    if quarter % lanes:
        def one(weight):
            padded = jnp.pad(weight.reshape(rows, owners, per), ((0, 0), (0, 0), (0, 4 * quarter - per)))
            return lax.dynamic_slice_in_dim(padded, s * quarter, quarter, 2).reshape(rows, owners * quarter)

        return jnp.concatenate([one(gate), one(up)], axis=1)
    return pl.pallas_call(
        functools.partial(pick_kernel, owners=owners, per=per, quarter=quarter),
        out_shape=jax.ShapeDtypeStruct((rows, 2 * owners * quarter), gate.dtype),
        grid_spec=pltpu.PrefetchScalarGridSpec(
            num_scalar_prefetch=1,
            grid=(1,),
            in_specs=[pl.BlockSpec(gate.shape, lambda i, s: (0, 0))] * 2,
            out_specs=pl.BlockSpec((rows, 2 * owners * quarter), lambda i, s: (0, 0)),
        ),
        name="pick_columns",
    )(s.reshape(1), gate, up)


def place_kernel(parts_ref, gate_ref, up_ref, *, owners, per, quarter):
    for half, ref in enumerate((gate_ref, up_ref)):
        for d in range(owners):
            pieces = []
            for choice in range(4):
                width = min(quarter, per - choice * quarter)
                at = (half * owners + d) * quarter
                pieces.append(parts_ref[choice, :, at : at + width].astype(wide))
            ref[:, d * per : (d + 1) * per] = jnp.concatenate(pieces, axis=1)


def place_columns(parts, total):
    owners = lax.axis_size("dp")
    rows = parts.shape[1]
    per = total // owners
    quarter = quarter_of(per)
    if quarter % lanes:
        grid = parts.reshape(4, rows, 2, owners, quarter).transpose(2, 1, 3, 0, 4)
        flat = grid.reshape(2, rows, owners, 4 * quarter)[:, :, :, :per].reshape(2, rows, total)
        return (flat[0].astype(wide), flat[1].astype(wide))
    block = 96 if rows % 96 == 0 else rows
    return pl.pallas_call(
        functools.partial(place_kernel, owners=owners, per=per, quarter=quarter),
        out_shape=[jax.ShapeDtypeStruct((rows, total), wide)] * 2,
        grid=(rows // block,),
        in_specs=[pl.BlockSpec((4, block, parts.shape[2]), lambda i: (0, i, 0))],
        out_specs=[pl.BlockSpec((block, total), lambda i: (i, 0))] * 2,
        name="place_columns",
    )(parts)


def slot_index(slot, s):
    return s ^ (2 * (slot % 2) + slot // 2)


def toeplitz_kernel(offsets_ref, out_ref, *, block, heads):
    for head in range(heads):
        row = jnp.broadcast_to(offsets_ref[head : head + 1, :], (block, offsets_ref.shape[1]))
        width = row.shape[1]
        rolled = pltpu.roll(row, width - block, 1, stride=1, stride_axis=0)
        out_ref[head] = rolled[:, : width - block]


def toeplitz(per_offset, block):
    heads, width = per_offset.shape
    return pl.pallas_call(
        functools.partial(toeplitz_kernel, block=block, heads=heads),
        out_shape=jax.ShapeDtypeStruct((heads, block, width - block), wide),
        name="toeplitz",
    )(per_offset)


def forward_kernel(s_ref, rows_ref, all_ref, bias_ref, out_ref, probs_ref, *, heads, size, block):
    s = s_ref[0]
    here = slot_index(pl.program_id(0), s)
    inner = heads * size
    outs = []
    for head in range(heads):
        query = rows_ref[:, head * size : (head + 1) * size]
        key = all_ref[:, inner + head * size : inner + (head + 1) * size]
        value = all_ref[:, 2 * inner + head * size : 2 * inner + (head + 1) * size]
        scores = lax.dot_general(query, key, (((1,), (1,)), ((), ())), preferred_element_type=wide)
        pieces = []
        for slot in range(4):
            start = pl.multiple_of((slot_index(slot, s) - here + 3) * block, block)
            pieces.append(scores[:, slot * block : (slot + 1) * block] + bias_ref[head, :, pl.ds(start, block)])
        scores = jnp.concatenate(pieces, axis=1)
        expo = jnp.exp(scores - jnp.max(scores, axis=-1, keepdims=True))
        probs = (expo * (1.0 / jnp.sum(expo, axis=-1, keepdims=True))).astype(low)
        probs_ref[head] = probs
        outs.append(jnp.dot(probs, value, preferred_element_type=wide))
    out_ref[...] = jnp.concatenate(outs, axis=1).astype(low)


def attend_forward(mixed, bias, s, heads):
    length, columns = mixed.shape
    inner = columns // 3
    block = length // 4
    return pl.pallas_call(
        functools.partial(forward_kernel, heads=heads, size=inner // heads, block=block),
        out_shape=[
            jax.ShapeDtypeStruct((length, inner), low),
            jax.ShapeDtypeStruct((heads, length, length), low),
        ],
        grid_spec=pltpu.PrefetchScalarGridSpec(
            num_scalar_prefetch=1,
            grid=(4,),
            in_specs=[
                pl.BlockSpec((block, columns), lambda i, s: (i, 0)),
                pl.BlockSpec((length, columns), lambda i, s: (0, 0)),
                pl.BlockSpec(bias.shape, lambda i, s: (0, 0, 0)),
            ],
            out_specs=[
                pl.BlockSpec((block, inner), lambda i, s: (i, 0)),
                pl.BlockSpec((heads, block, length), lambda i, s: (0, i, 0)),
            ],
        ),
        cost_estimate=pl.CostEstimate(
            flops=16 * length * length * inner, transcendentals=heads * length * length,
            bytes_accessed=2 * heads * length * length + bias.size * 4,
        ),
        name="attend_forward",
    )(s.reshape(1), mixed, mixed, bias)


def backward_kernel(
    s_ref, rows_ref, all_ref, grad_ref, probs_ref, out_ref, sums_ref, key_ref, value_ref, *, heads, size, block
):
    s = s_ref[0]
    step = pl.program_id(0)
    here = slot_index(step, s)
    inner = heads * size

    @pl.when(step == 0)
    def _():
        sums_ref[...] = jnp.zeros_like(sums_ref)
        key_ref[...] = jnp.zeros_like(key_ref)
        value_ref[...] = jnp.zeros_like(value_ref)

    outs = []
    for head in range(heads):
        query = rows_ref[:, head * size : (head + 1) * size]
        key = all_ref[:, inner + head * size : inner + (head + 1) * size]
        value = all_ref[:, 2 * inner + head * size : 2 * inner + (head + 1) * size]
        grad = grad_ref[:, head * size : (head + 1) * size]
        probs_low = probs_ref[head]
        probs = probs_low.astype(wide)
        prob_grad = lax.dot_general(grad, value, (((1,), (1,)), ((), ())), preferred_element_type=wide)
        centred = jnp.sum(probs * prob_grad, axis=-1, keepdims=True)
        score_low = (probs * (prob_grad - centred)).astype(low)
        outs.append(jnp.dot(score_low, key, preferred_element_type=wide))
        key_ref[head] += lax.dot_general(query, score_low, (((0,), (0,)), ((), ())), preferred_element_type=wide)
        value_ref[head] += lax.dot_general(grad, probs_low, (((0,), (0,)), ((), ())), preferred_element_type=wide)
        for slot in range(4):
            start = pl.multiple_of((slot_index(slot, s) - here + 3) * block, block)
            sums_ref[head, :, pl.ds(start, block)] += score_low[:, slot * block : (slot + 1) * block].astype(wide)
    at = pl.multiple_of(step * block, block)
    out_ref[pl.ds(at, block), :inner] = jnp.concatenate(outs, axis=1).astype(low)

    @pl.when(step == 3)
    def _():
        turned = [key_ref[head].T for head in range(heads)] + [value_ref[head].T for head in range(heads)]
        out_ref[:, inner:] = jnp.concatenate(turned, axis=1).astype(low)


def attend_backward(mixed, grad, probs, s, heads):
    length, columns = mixed.shape
    inner = columns // 3
    block = length // 4
    size = inner // heads
    return pl.pallas_call(
        functools.partial(backward_kernel, heads=heads, size=size, block=block),
        out_shape=[
            jax.ShapeDtypeStruct((length, columns), low),
            jax.ShapeDtypeStruct((heads, block, 2 * length - block), wide),
        ],
        grid_spec=pltpu.PrefetchScalarGridSpec(
            num_scalar_prefetch=1,
            grid=(4,),
            in_specs=[
                pl.BlockSpec((block, columns), lambda i, s: (i, 0)),
                pl.BlockSpec((length, columns), lambda i, s: (0, 0)),
                pl.BlockSpec((block, inner), lambda i, s: (i, 0)),
                pl.BlockSpec((heads, block, length), lambda i, s: (0, i, 0)),
            ],
            out_specs=[
                pl.BlockSpec((length, columns), lambda i, s: (0, 0)),
                pl.BlockSpec((heads, block, 2 * length - block), lambda i, s: (0, 0, 0)),
            ],
            scratch_shapes=[pltpu.VMEM((heads, size, length), wide), pltpu.VMEM((heads, size, length), wide)],
        ),
        cost_estimate=pl.CostEstimate(
            flops=32 * length * length * inner, transcendentals=0,
            bytes_accessed=2 * heads * length * length + heads * block * length * 8,
        ),
        name="attend_backward",
    )(s.reshape(1), mixed, mixed, grad, probs)


def diagonal_kernel(*refs, heads, block):
    out_ref = refs[-1]
    width = refs[0].shape[2] + block
    for head in range(heads):
        total = refs[0][head]
        for ref in refs[1:-1]:
            total = total + ref[head]
        total = jnp.concatenate([total, jnp.zeros((block, block), wide)], axis=1)
        rows = block
        while rows > 8:
            rows //= 2
            total = total[:rows] + pltpu.roll(total[rows:], width - rows, 1)
        total = pltpu.roll(total, block, 1)
        line = total[0:1]
        for row in range(1, 8):
            line = line + pltpu.roll(total[row : row + 1], width - row, 1)
        out_ref[head : head + 1, :] = line


def diagonal_sums(sums):
    heads, block, width = sums[0].shape
    return pl.pallas_call(
        functools.partial(diagonal_kernel, heads=heads, block=block),
        out_shape=jax.ShapeDtypeStruct((heads, width + block), wide),
        name="diagonal_sums",
    )(*sums)


def ffn_kernel(x_ref, g_ref, gu_ref, down_ref, hidden_ref, grads_ref, *, width, tile):
    x = x_ref[...]
    g = g_ref[...]
    for start in range(0, width, tile):
        gate_pre = jnp.dot(x, gu_ref[:, start : start + tile], preferred_element_type=wide)
        up_pre = jnp.dot(x, gu_ref[:, width + start : width + start + tile], preferred_element_type=wide)
        hidden_grad = lax.dot_general(
            g, down_ref[start : start + tile, :], (((1,), (1,)), ((), ())), preferred_element_type=wide
        )
        gelu_value, gelu_slope = gelu_pair(gate_pre)
        hidden_ref[:, start : start + tile] = (gelu_value * up_pre).astype(low)
        grads_ref[:, start : start + tile] = (hidden_grad * up_pre * gelu_slope).astype(low)
        grads_ref[:, width + start : width + start + tile] = (hidden_grad * gelu_value).astype(low)


def feed_forward(x, g, gate_up, down):
    tokens, model = x.shape
    width = down.shape[0]
    rows = 256
    tile = 256
    return pl.pallas_call(
        functools.partial(ffn_kernel, width=width, tile=tile),
        out_shape=[
            jax.ShapeDtypeStruct((tokens, width), low),
            jax.ShapeDtypeStruct((tokens, 2 * width), low),
        ],
        grid=(tokens // rows,),
        in_specs=[
            pl.BlockSpec((rows, model), lambda i: (i, 0)),
            pl.BlockSpec((rows, model), lambda i: (i, 0)),
            pl.BlockSpec((model, 2 * width), lambda i: (0, 0)),
            pl.BlockSpec((width, model), lambda i: (0, 0)),
        ],
        out_specs=[
            pl.BlockSpec((rows, width), lambda i: (i, 0)),
            pl.BlockSpec((rows, 2 * width), lambda i: (i, 0)),
        ],
        cost_estimate=pl.CostEstimate(
            flops=6 * tokens * model * width, transcendentals=tokens * width,
            bytes_accessed=2 * (2 * tokens * model + 3 * model * width + 3 * tokens * width),
        ),
        name="feed_forward",
    )(x, g, gate_up, down)


def per_device(
    tokens,
    query_weight,
    key_weight,
    value_weight,
    mix_weight,
    gate_weight,
    up_weight,
    down_weight,
    attn_gain,
    ffn_gain,
    bias_table,
    bucket_ids,
    out_grad,
):
    owners = lax.axis_size("dp")
    s = lax.axis_index("seq")
    core = s % 2
    micro_count = tokens.shape[0]
    local, model = tokens.shape[2:]
    bucket_count, heads = bias_table.shape
    length = bucket_ids.shape[0] // 2
    hidden_total = gate_weight.shape[1]
    per = down_weight.shape[0]
    quarter = quarter_of(per)
    width = owners * quarter
    inner = query_weight.shape[1] // 4
    mix_rows = mix_weight.shape[0]

    shard_rows = query_weight.shape[0]
    own_heads = [lax.dynamic_slice_in_dim(w, s * inner, inner, 1) for w in (query_weight, key_weight, value_weight)]
    gains = jnp.pad(jnp.stack([attn_gain, ffn_gain], axis=1), ((0, 0), (0, 62)))
    qkv_gathered = gather_dp(jnp.concatenate(own_heads + [gains], axis=1)).reshape(model, 3 * inner + 64)
    full_qkv = qkv_gathered[:, : 3 * inner]
    gain_one = qkv_gathered[:, 3 * inner].astype(wide)
    gain_two = qkv_gathered[:, 3 * inner + 1].astype(wide)
    mix_half = gather_dp(lax.dynamic_slice_in_dim(mix_weight, core * (mix_rows // 2), mix_rows // 2, 0))
    mix_other = flip_core(mix_half)
    full_mix = jnp.stack(
        [jnp.where(core == 0, mix_half, mix_other), jnp.where(core == 0, mix_other, mix_half)], axis=1
    ).reshape(4, inner, model)
    slot_mix = by_slot(full_mix, s).reshape(4 * inner, model)
    full_gu = gather_dp(pick_columns(gate_weight, up_weight, s)).reshape(model, 2 * width)
    down_padded = jnp.pad(down_weight, ((0, 4 * quarter - per), (0, 0)))
    full_down = gather_dp(lax.dynamic_slice_in_dim(down_padded, s * quarter, quarter, 0)).reshape(width, model)

    onehot = (jnp.arange(bucket_count, dtype=jnp.int32)[:, None] == bucket_ids[None, :]).astype(wide)
    per_offset = lax.dot_general(
        bias_table, onehot, (((0,), (0,)), ((), ())), precision=lax.Precision.HIGHEST
    )
    bias = toeplitz(per_offset, local)

    saved = []
    for micro in range(micro_count):
        x = gather_seq(tokens[micro, 0]).reshape(length, model)
        features = x.astype(wide)
        normed, inverse = rms_forward(features)
        normed_low = (normed * gain_one).astype(low)
        mixed = mm(normed_low, full_qkv, (1, 0))
        attended, probs = attend_forward(mixed, bias, s, heads)
        blocks = attended.reshape(4, local, inner)
        from_y = flip_y(blocks)[jnp.array([1, 0, 3, 2])]
        from_core = flip_core(jnp.stack([blocks, from_y]))[:, jnp.array([2, 3, 0, 1])]
        attended_all = jnp.concatenate(
            [blocks, from_y, from_core[0], from_core[1]], axis=2
        ).reshape(length, 4 * inner)
        middle = features + mm(attended_all, slot_mix, (1, 0), wide)
        normed_middle, inverse_middle = rms_forward(middle)
        ffn_low = (normed_middle * gain_two).astype(low)
        saved.append((x, normed_low, mixed, probs, attended_all[:local], middle[:local], ffn_low))

    outputs, middle_grads, grads, hiddens, cotangents = [], [], [], [], []
    ffn_gain_sum = jnp.zeros((model,), wide)
    mix_ins, qkv_grads, diagonals, hidden_grads = [], [], [], []
    for micro in range(micro_count):
        x, normed_low, mixed, probs, attended_own, middle_own, ffn_low = saved[micro]
        g = gather_seq(out_grad[micro, 0]).reshape(length, model)
        hidden, hidden_grad = feed_forward(ffn_low, g, full_gu, full_down)
        ffn_in = scatter_seq(mm(hidden_grad, full_gu, (1, 1)).reshape(4, local, model))
        normed_middle, inverse_middle = rms_forward(middle_own)
        middle_grad = out_grad[micro, 0].astype(wide) + rms_backward(
            ffn_in, normed_middle, inverse_middle, gain_two
        )
        ffn_gain_sum = ffn_gain_sum + jnp.sum(ffn_in * normed_middle, axis=0)
        mix_in = middle_grad.astype(low)
        result = scatter_seq(mm(hidden, full_down, (1, 0)).reshape(4, local, model))
        outputs.append((middle_own + result).astype(low))
        attended_grad = mm(mix_in, slot_mix, (1, 1))
        far = flip_y(jnp.stack([attended_grad[:, inner : 2 * inner], attended_grad[:, 3 * inner :]]))
        near = flip_core(jnp.stack([attended_grad[:, 2 * inner : 3 * inner], far[1]]))
        own_grad = jnp.concatenate([attended_grad[:, :inner], far[0], near[0], near[1]], axis=0)
        qkv_grad, diagonal = attend_backward(mixed, own_grad, probs, s, heads)
        hiddens.append(hidden)
        hidden_grads.append(hidden_grad)
        cotangents.append(g)
        middle_grads.append(middle_grad)
        mix_ins.append(mix_in)
        qkv_grads.append(qkv_grad)
        diagonals.append(diagonal)

    all_ffn_low = jnp.concatenate([item[6] for item in saved])
    all_normed = jnp.concatenate([item[1] for item in saved])
    all_attended = jnp.concatenate([item[4] for item in saved])
    grad_gu = scatter_dp(mm(all_ffn_low, jnp.concatenate(hidden_grads), (0, 0)).reshape(owners, shard_rows, 2 * width))
    grad_down = scatter_dp(
        mm(jnp.concatenate(hiddens), jnp.concatenate(cotangents), (0, 0)).reshape(owners, quarter, model)
    )
    grad_mix = by_index(mm(all_attended, jnp.concatenate(mix_ins), (0, 0)).reshape(4, inner, model), s)
    grad_mix = grad_mix.reshape(owners, 2, mix_rows // 2, model)
    kept = lax.dynamic_index_in_dim(grad_mix, core, 1, keepdims=False)
    sent = lax.dynamic_index_in_dim(grad_mix, 1 - core, 1, keepdims=False)
    grad_mix = scatter_dp((kept.astype(wide) + flip_core(sent).astype(wide)).astype(low)).astype(low)

    input_grads = []
    attn_gain_sum = jnp.zeros((model,), wide)
    for micro in range(micro_count):
        x = saved[micro][0]
        partial = mm(qkv_grads[micro], full_qkv, (1, 1))
        normed, inverse = rms_forward(x.astype(wide))
        attn_gain_sum = attn_gain_sum + jnp.sum(partial.astype(wide) * normed, axis=0)
        attn_in = scatter_seq(partial.reshape(4, local, model))
        input_grads.append(
            middle_grads[micro] + rms_backward(attn_in, normed[:local], inverse[:local], gain_one)
        )
    gain_sums = jnp.pad(jnp.stack([attn_gain_sum, ffn_gain_sum], axis=1).astype(low), ((0, 0), (0, 62)))
    grad_qkv = scatter_dp(
        jnp.concatenate(
            [mm(all_normed, jnp.concatenate(qkv_grads), (0, 0)), gain_sums], axis=1
        ).reshape(owners, shard_rows, 3 * inner + 64)
    )

    grad_gate, grad_up = place_columns(by_index(gather_seq(grad_gu.astype(low)), s), hidden_total)
    grad_down = by_index(gather_seq(grad_down.astype(low)), s).reshape(4 * quarter, model)[:per].astype(wide)
    mix_sum = (grad_mix.astype(wide) + flip_y(grad_mix).astype(wide)).astype(low)
    mix_two = flip_core(mix_sum)
    grad_mix = jnp.concatenate(
        [jnp.where(core == 0, mix_sum, mix_two), jnp.where(core == 0, mix_two, mix_sum)]
    ).astype(wide)
    qkv_parts = by_index(gather_seq(grad_qkv.astype(low)), s).astype(wide)
    grad_query, grad_key, grad_value = (
        jnp.concatenate([qkv_parts[i, :, k * inner : (k + 1) * inner] for i in range(4)], axis=1) for k in range(3)
    )
    grad_gains = jnp.sum(qkv_parts[:, :, 3 * inner : 3 * inner + 2], axis=0)
    table_local = lax.dot_general(
        onehot, diagonal_sums(diagonals), (((1,), (1,)), ((), ())), precision=lax.Precision.HIGHEST
    )
    grad_bias_table = sum_dp(table_local)
    return (
        jnp.stack(outputs)[:, None],
        jnp.stack(input_grads)[:, None],
        grad_query,
        grad_key,
        grad_value,
        grad_mix,
        grad_gate,
        grad_up,
        grad_down,
        grad_gains[:, 0],
        grad_gains[:, 1],
        grad_bias_table,
    )


def solution(mesh):
    in_specs = (
        P(None, "dp", "seq", None),
        P("dp", None),
        P("dp", None),
        P("dp", None),
        P("dp", None),
        P("dp", None),
        P("dp", None),
        P("dp", None),
        P("dp"),
        P("dp"),
        P(None, "seq"),
        P(),
        P(None, "dp", "seq", None),
    )
    out_specs = (
        P(None, "dp", "seq", None),
        P(None, "dp", "seq", None),
        P("dp", None),
        P("dp", None),
        P("dp", None),
        P("dp", None),
        P("dp", None),
        P("dp", None),
        P("dp", None),
        P("dp"),
        P("dp"),
        P(None, "seq"),
    )
    return jax.shard_map(
        per_device, mesh=mesh, in_specs=in_specs, out_specs=out_specs, check_vma=False
    )
```

time: 3270 us -> 939 us (0.29)
  local copies, waits for them, and re-layouts: 1130 us -> 96.7 us
  waiting for transfers between devices: 1350 us -> 337 us
  matrix products: 368 us -> 114 us
  starting transfers between devices: 63.2 us -> 179 us
  Pallas kernels: 0 us -> 109 us
  other arithmetic: 182 us -> 88.6 us
  loops' own time: 70.7 us -> 0 us
  blocking collectives: 66.8 us -> 0 us
    reduce_scatter x7 -> x0, waiting for transfers between devices: 1270 us -> none  [the longest x1 394 us: reduce_grads(): lax.psum_scatter(g_gate, 'dp', scatter_dimension=0, tiled=True)]
    unnamed x220 -> x179, local copies, waits for them, and re-layouts: 594 us -> 5.9 us
    ppermute x0 -> x109, waiting for transfers between devices: none -> 337 us  [the longest x20 159 us: flip_x(): return lax.ppermute(array, 'dp', [(d, d ^ 1) for d in range(8)])]
    dot_general x72 -> x18, matrix products: 368 us -> 114 us  [the longest x16 113 us: mm(): lax.dot_general(left, right, ((dims[:1], dims[1:]), ((), ())), preferred_...]
    while x62 -> x0, local copies, waits for them, and re-layouts: 222 us -> none
    ppermute x0 -> x109, starting transfers between devices: none -> 179 us  [the longest x24 98.2 us: z_up(): lax.ppermute(array, 'dp', [(2 * z + x, 2 * z + 2 + x) for z in sources fo...]
    rev x4 -> x0, local copies, waits for them, and re-layouts: 122 us -> none  [offset_sums(): flipped = jnp.flip(score_grad, axis=1).astype(jnp.float32)]
    reshape x5 -> x3, local copies, waits for them, and re-layouts: 115 us -> 4.08 us  [the longest x2 3.98 us: per_device(): blocks = attended.reshape(4, local, inner)]
  transfers between devices with their start and end apart: 31 -> 109, of which waited for: 13 -> 33; matrix products, arithmetic and copies ran while one was open for 47% -> 22% of each run, Pallas kernels for 0% -> 8%
where the time goes in v1:
time: 939 us; the launch traced here: 928 us
  waiting for transfers between devices  337 us (36%)
  starting transfers between devices  179 us (19%)
  matrix products  114 us (12%)
  Pallas kernels  109 us (12%)
  local copies, waits for them, and re-layouts  96.7 us (10%)
  other arithmetic  88.6 us (9%)
    ppermute x20, waiting for transfers between devices, flip_x(): return lax.ppermute(array, 'dp', [(d, d ^ 1) for d in range(8)])  159 us
    dot_general x16, matrix products, mm(): lax.dot_general(left, right, ((dims[:1], dims[1:]), ((), ())), preferred_...  113 us
    ppermute x24, starting transfers between devices, z_up(): lax.ppermute(array, 'dp', [(2 * z + x, 2 * z + 2 + x) for z in sources fo...  98.2 us
    ppermute x18, waiting for transfers between devices, flip_y(): return lax.ppermute(array, 'seq', [(0, 2), (2, 0), (1, 3), (3, 1)])  76.4 us
    ppermute x24, waiting for transfers between devices, z_down(): lax.ppermute(array, 'dp', [(2 * z + x, 2 * z - 2 + x) for z in sources fo...  61.1 us
    ppermute x24, waiting for transfers between devices, z_up(): lax.ppermute(array, 'dp', [(2 * z + x, 2 * z + 2 + x) for z in sources fo...  39.9 us
    pallas_call x2, Pallas kernels, feed_forward(): pl.pallas_call(functools.partial(ffn_kernel, width=width, tile=tile), out...  32.5 us
    pallas_call x2, Pallas kernels, attend_backward(): pl.pallas_call(functools.partial(backward_kernel, heads=heads, size=size,...  32.2 us
  transfers between devices with their start and end apart: 109, of which 33 were waited for; matrix products, arithmetic and copies ran while one was open for 22% of the time, Pallas kernels for 8%

profile of v1, /device:TPU:0, one launch (start us, length us, event | category | flops | bytes accessed | tf_op | source)
XLA Modules:
  0.0 928.2 jit_solution(2459719647243466723)
XLA Ops:
  52.0 22.3 %collective-permute-done.17 = bf16[48,1536]{1,0:T(8,128)(2,1)S(1)} collective-permute-done((bf16[48,1536]{1,0:T(8,128)(2,1)S(1)}, bf16[48,1536]{1,0:T(8,128)(2,1)S(1)}, u32[]{:S(2)}, u32[]{:S(2)}) %collective-permute-start.17) | collective-permute-done | bytes 147488 | tf_op jit(solution)/shard_map/ppermute | solution.py:51
  128.1 13.0 %collective-permute-done.49 = bf16[256,1536]{1,0:T(8,128)(2,1)S(1)} collective-permute-done((bf16[256,1536]{1,0:T(8,128)(2,1)S(1)}, bf16[256,1536]{1,0:T(8,128)(2,1)S(1)}, u32[]{:S(2)}, u32[]{:S(2)}) %collective-permute-start.49) | collective-permute-done | bytes 786464 | tf_op jit(solution)/shard_map/ppermute | solution.py:47
  141.9 14.3 %collective-permute-done.25 = bf16[256,1536]{1,0:T(8,128)(2,1)S(1)} collective-permute-done((bf16[256,1536]{1,0:T(8,128)(2,1)S(1)}, bf16[256,1536]{1,0:T(8,128)(2,1)S(1)}, u32[]{:S(2)}, u32[]{:S(2)}) %collective-permute-start.25) | collective-permute-done | bytes 786464 | tf_op jit(solution)/shard_map/ppermute | solution.py:47
  164.0 11.4 %collective-permute-done.43 = bf16[128,1536]{1,0:T(8,128)(2,1)S(1)} collective-permute-done((bf16[128,1536]{1,0:T(8,128)(2,1)S(1)}, bf16[128,1536]{1,0:T(8,128)(2,1)S(1)}, u32[]{:S(2)}, u32[]{:S(2)}) %collective-permute-start.43) | collective-permute-done | bytes 393248 | tf_op jit(solution)/shard_map/ppermute | solution.py:51
  183.1 22.1 %collective-permute-done.46 = bf16[128,1536]{1,0:T(8,128)(2,1)S(1)} collective-permute-done((bf16[128,1536]{1,0:T(8,128)(2,1)S(1)}, bf16[128,1536]{1,0:T(8,128)(2,1)S(1)}, u32[]{:S(2)}, u32[]{:S(2)}) %collective-permute-start.46) | collective-permute-done | bytes 393248 | tf_op jit(solution)/shard_map/ppermute | solution.py:51
  229.4 12.9 %attend_forward.2 = (bf16[1024,192]{1,0:T(8,128)(2,1)}, bf16[3,1024,1024]{2,1,0:T(8,128)(2,1)}) custom-call(s32[1]{0:T(128)} %bitcast.4.s_ref, bf16[1024,576]{1,0:T(8,128)(2,1)} %convolution_convert_fusion.8.rows_ref.all_ref, bf16[1024,576]{1,0:T(8,128)(2,1)} %convolution_convert_fusion.8.rows_ref.all_ref, f32[3,256,1792]{2,1,0:T(8,128)} %toeplitz.1.bias_ref), custom_call_target="tpu_custom_call" | custom-call | flops 3221225472 | bytes 11796480 | tf_op jit(solution)/shard_map/attend_forward/pallas_call | solution.py:275
  247.5 14.3 %collective-permute-done.34 = bf16[192,2048]{1,0:T(8,128)(2,1)} collective-permute-done((bf16[192,2048]{1,0:T(8,128)(2,1)}, bf16[192,2048]{1,0:T(8,128)(2,1)}, u32[]{:S(2)}, u32[]{:S(2)}) %collective-permute-start.34) | collective-permute-done | bytes 786464 | tf_op jit(solution)/shard_map/ppermute | solution.py:59
  268.7 13.2 %attend_forward.3 = (bf16[1024,192]{1,0:T(8,128)(2,1)}, bf16[3,1024,1024]{2,1,0:T(8,128)(2,1)}) custom-call(s32[1]{0:T(128)} %bitcast.4.s_ref, bf16[1024,576]{1,0:T(8,128)(2,1)} %convolution_convert_fusion.7.rows_ref.all_ref, bf16[1024,576]{1,0:T(8,128)(2,1)} %convolution_convert_fusion.7.rows_ref.all_ref, f32[3,256,1792]{2,1,0:T(8,128)} %toeplitz.1.bias_ref), custom_call_target="tpu_custom_call" | custom-call | flops 3221225472 | bytes 11796480 | tf_op jit(solution)/shard_map/attend_forward/pallas_call | solution.py:275
  323.2 8.7 multiply_reduce_fusion.3
  350.9 16.2 %feed_forward.2 = (bf16[1024,1024]{1,0:T(8,128)(2,1)}, bf16[1024,2048]{1,0:T(8,128)(2,1)}) custom-call(bf16[1024,1536]{1,0:T(8,128)(2,1)} %get-tuple-element.210.x_ref, bf16[1024,1536]{1,0:T(8,128)(2,1)} %bitcast.494, bf16[1536,2048]{1,0:T(8,128)(2,1)} %bitcast.48.gu_ref, bf16[1024,1536]{1,0:T(8,128)(2,1)} %bitcast.57.down_ref), custom_call_target="tpu_custom_call" | custom-call | flops 9663676416 | bytes 22020096 | tf_op jit(solution)/shard_map/feed_forward/pallas_call | solution.py:424
  367.2 11.4 %convolution_convert_fusion.1 = bf16[1024,1536]{1,0:T(8,128)(2,1)} fusion(bf16[1024,2048]{1,0:T(8,128)(2,1)} %get-tuple-element.30, bf16[1536,2048]{1,0:T(8,128)(2,1)} %bitcast.48.gu_ref), kind=kOutput, calls=%fused_computation.44 | convolution fusion | flops 6444023808 | bytes 13631488 | tf_op jit(solution)/shard_map/dot_general | solution.py:39
  378.5 16.2 %feed_forward.3 = (bf16[1024,1024]{1,0:T(8,128)(2,1)}, bf16[1024,2048]{1,0:T(8,128)(2,1)}) custom-call(bf16[1024,1536]{1,0:T(8,128)(2,1)} %get-tuple-element.211.x_ref, bf16[1024,1536]{1,0:T(8,128)(2,1)} %bitcast.496, bf16[1536,2048]{1,0:T(8,128)(2,1)} %bitcast.48.gu_ref, bf16[1024,1536]{1,0:T(8,128)(2,1)} %bitcast.57.down_ref), custom_call_target="tpu_custom_call" | custom-call | flops 9663676416 | bytes 22020096 | tf_op jit(solution)/shard_map/feed_forward/pallas_call | solution.py:424
  394.8 10.2 %convolution_convert_fusion = bf16[1024,1536]{1,0:T(8,128)(2,1)S(1)} fusion(bf16[1024,2048]{1,0:T(8,128)(2,1)} %get-tuple-element.33, bf16[1536,2048]{1,0:T(8,128)(2,1)} %bitcast.48.gu_ref), kind=kOutput, calls=%fused_computation.43 | convolution fusion | flops 6444023808 | bytes 13631488 | tf_op jit(solution)/shard_map/dot_general | solution.py:39
  405.0 16.0 %fusion.4 = bf16[1536,2048]{1,0:T(8,128)(2,1)S(1)} fusion(bf16[1024,2048]{1,0:T(8,128)(2,1)} %get-tuple-element.33, bf16[1024,2048]{1,0:T(8,128)(2,1)} %get-tuple-element.30, bf16[1024,1536]{1,0:T(8,128)(2,1)S(1)} %copy-done.42, bf16[1024,1536]{1,0:T(8,128)(2,1)S(1)} %copy-done.41), kind=kOutput, calls=%fused_computation.8 | convolution fusion | flops 12917407744 | bytes 20971520 | tf_op jit(solution)/shard_map/dot_general | solution.py:39
  421.0 9.9 %convolution_convert_fusion.5 = bf16[1024,1536]{1,0:T(8,128)(2,1)} fusion(bf16[1024,1024]{1,0:T(8,128)(2,1)} %get-tuple-element.27, bf16[1024,1536]{1,0:T(8,128)(2,1)} %bitcast.57.down_ref), kind=kOutput, calls=%fused_computation.49 | convolution fusion | flops 3222798336 | bytes 8388608 | tf_op jit(solution)/shard_map/dot_general | solution.py:39
  436.6 11.2 %fusion.24 = bf16[1024,1536]{1,0:T(8,128)(2,1)} fusion(bf16[1024,1536]{1,0:T(8,128)(2,1)S(1)} %bitcast.497, bf16[1024,1536]{1,0:T(8,128)(2,1)S(1)} %bitcast.495, bf16[1024,1024]{1,0:T(8,128)(2,1)} %get-tuple-element.29, bf16[1024,1024]{1,0:T(8,128)(2,1)} %get-tuple-element.27), kind=kOutput, calls=%fused_computation.47 | convolution fusion | flops 6464995328 | bytes 13631488 | tf_op jit(solution)/shard_map/dot_general | solution.py:39
  467.3 94.3 %collective-permute-done.97 = bf16[4,128,1536]{2,1,0:T(8,128)(2,1)S(1)} collective-permute-done((bf16[4,128,1536]{2,1,0:T(8,128)(2,1)S(1)}, bf16[4,128,1536]{2,1,0:T(8,128)(2,1)S(1)}, u32[]{:S(2)}, u32[]{:S(2)}) %collective-permute-start.97) | collective-permute-done | bytes 1572896 | tf_op jit(solution)/shard_map/ppermute | solution.py:51
  563.0 15.6 %collective-permute-start.98 = (bf16[128,1536]{1,0:T(8,128)(2,1)S(1)}, bf16[128,1536]{1,0:T(8,128)(2,1)S(1)}, u32[]{:S(2)}, u32[]{:S(2)}) collective-permute-start(bf16[128,1536]{1,0:T(8,128)(2,1)S(1)} %get-tuple-element.162), channel_id=1, source_target_pairs={{0,8},{4,12},{1,9},{5,13},{2,10},{6,14},{3,11},{7,15}} | collective-permute-start | bytes 1179656 | tf_op jit(solution)/shard_map/ppermute | solution.py:55
  579.7 6.9 collective-permute-done.98
  621.3 7.8 collective-permute-start.100
  632.0 16.2 %attend_backward.2 = (bf16[1024,576]{1,0:T(8,128)(2,1)}, f32[3,256,1792]{2,1,0:T(8,128)}) custom-call(s32[1]{0:T(128)} %bitcast.4.s_ref, bf16[1024,576]{1,0:T(8,128)(2,1)} %convolution_convert_fusion.8.rows_ref.all_ref, bf16[1024,576]{1,0:T(8,128)(2,1)} %convolution_convert_fusion.8.rows_ref.all_ref, bf16[1024,192]{1,0:T(8,128)(2,1)} %pad_maximum_fusion.20.grad_ref, ...), custom_call_target="tpu_custom_call" | custom-call | flops 6442450944 | bytes 12582912 | tf_op jit(solution)/shard_map/attend_backward/pallas_call | solution.py:347
  648.2 9.2 multiply_reduce_fusion.1
  659.3 16.1 %attend_backward.3 = (bf16[1024,576]{1,0:T(8,128)(2,1)}, f32[3,256,1792]{2,1,0:T(8,128)}) custom-call(s32[1]{0:T(128)} %bitcast.4.s_ref, bf16[1024,576]{1,0:T(8,128)(2,1)} %convolution_convert_fusion.7.rows_ref.all_ref, bf16[1024,576]{1,0:T(8,128)(2,1)} %convolution_convert_fusion.7.rows_ref.all_ref, bf16[1024,192]{1,0:T(8,128)(2,1)} %pad_maximum_fusion.21.grad_ref, ...), custom_call_target="tpu_custom_call" | custom-call | flops 6442450944 | bytes 12582912 | tf_op jit(solution)/shard_map/attend_backward/pallas_call | solution.py:347
  675.4 8.3 multiply_reduce_fusion
  683.7 6.6 diagonal_sums.1
  739.4 8.0 collective-permute-done.104
  793.0 9.2 collective-permute-done.81
  805.0 10.0 %collective-permute-start.82 = (bf16[48,1536]{1,0:T(8,128)(2,1)S(1)}, bf16[48,1536]{1,0:T(8,128)(2,1)S(1)}, u32[]{:S(2)}, u32[]{:S(2)}) collective-permute-start(bf16[48,1536]{1,0:T(8,128)(2,1)S(1)} %get-tuple-element.184), channel_id=1, source_target_pairs={{0,8},{4,12},{8,16},{12,20},{16,24},{20,28},{1,9},{5,13},{9,17},{1... | collective-permute-start | bytes 442376 | tf_op jit(solution)/shard_map/ppermute | solution.py:55
  831.1 18.5 %collective-permute-done.86 = bf16[48,1536]{1,0:T(8,128)(2,1)S(1)} collective-permute-done((bf16[48,1536]{1,0:T(8,128)(2,1)S(1)}, bf16[48,1536]{1,0:T(8,128)(2,1)S(1)}, u32[]{:S(2)}, u32[]{:S(2)}) %collective-permute-start.86) | collective-permute-done | bytes 147488 | tf_op jit(solution)/shard_map/ppermute | solution.py:47
  864.0 10.1 %collective-permute-done.91 = bf16[192,2048]{1,0:T(8,128)(2,1)S(1)} collective-permute-done((bf16[192,2048]{1,0:T(8,128)(2,1)S(1)}, bf16[192,2048]{1,0:T(8,128)(2,1)S(1)}, u32[]{:S(2)}, u32[]{:S(2)}) %collective-permute-start.91) | collective-permute-done | bytes 786464 | tf_op jit(solution)/shard_map/ppermute | solution.py:55
  874.1 20.8 %collective-permute-done.94 = bf16[192,2048]{1,0:T(8,128)(2,1)S(1)} collective-permute-done((bf16[192,2048]{1,0:T(8,128)(2,1)S(1)}, bf16[192,2048]{1,0:T(8,128)(2,1)S(1)}, u32[]{:S(2)}, u32[]{:S(2)}) %collective-permute-start.94) | collective-permute-done | bytes 786464 | tf_op jit(solution)/shard_map/ppermute | solution.py:59
  899.9 14.0 %collective-permute-done.95 = bf16[192,2048]{1,0:T(8,128)(2,1)S(1)} collective-permute-done((bf16[192,2048]{1,0:T(8,128)(2,1)S(1)}, bf16[192,2048]{1,0:T(8,128)(2,1)S(1)}, u32[]{:S(2)}, u32[]{:S(2)}) %collective-permute-start.95) | collective-permute-done | bytes 786464 | tf_op jit(solution)/shard_map/ppermute | solution.py:47
  (594 shorter events, 430.3 us)
Async XLA Ops:
  3.5 34.9 %collective-permute-start.14 = (bf16[48,1536]{1,0:T(8,128)(2,1)}, bf16[48,1536]{1,0:T(8,128)(2,1)}, u32[]{:S(2)}, u32[]{:S(2)}) collective-permute-start(bf16[48,1536]{1,0:T(8,128)(2,1)} %get-tuple-element.135), channel_id=1, source_target_pairs={{0,4},{4,0},{8,12},{12,8},{16,20},{20,16},{24,28},{28,24},{1,5},{5... | collective-permute-start | bytes 442376 | tf_op jit(solution)/shard_map/ppermute | solution.py:51
  6.4 38.2 %collective-permute-start.15 = (bf16[48,1536]{1,0:T(8,128)(2,1)}, bf16[48,1536]{1,0:T(8,128)(2,1)S(1)}, u32[]{:S(2)}, u32[]{:S(2)}) collective-permute-start(bf16[48,1536]{1,0:T(8,128)(2,1)} %get-tuple-element.135), channel_id=1, source_target_pairs={{8,0},{12,4},{16,8},{20,12},{24,16},{28,20},{9,1},{13,5},{17,9},{2... | collective-permute-start | bytes 442376 | tf_op jit(solution)/shard_map/ppermute | solution.py:59
  7.7 38.8 %collective-permute-start.16 = (bf16[48,1536]{1,0:T(8,128)(2,1)}, bf16[48,1536]{1,0:T(8,128)(2,1)}, u32[]{:S(2)}, u32[]{:S(2)}) collective-permute-start(bf16[48,1536]{1,0:T(8,128)(2,1)} %get-tuple-element.135), channel_id=1, source_target_pairs={{0,8},{4,12},{8,16},{12,20},{16,24},{20,28},{1,9},{5,13},{9,17},{1... | collective-permute-start | bytes 442376 | tf_op jit(solution)/shard_map/ppermute | solution.py:55
  44.6 81.1 %collective-permute-start.27 = (bf16[192,2048]{1,0:T(8,128)(2,1)}, bf16[192,2048]{1,0:T(8,128)(2,1)S(1)}, u32[]{:S(2)}, u32[]{:S(2)}) collective-permute-start(bf16[192,2048]{1,0:T(8,128)(2,1)} %pick_columns.1), channel_id=1, source_target_pairs={{0,4},{4,0},{8,12},{12,8},{16,20},{20,16},{24,28},{28,24},{1,5},{5... | collective-permute-start | bytes 2359304 | tf_op jit(solution)/shard_map/ppermute | solution.py:51
  46.5 37.3 %collective-permute-start.37 = (bf16[128,1536]{1,0:T(8,128)(2,1)}, bf16[128,1536]{1,0:T(8,128)(2,1)S(1)}, u32[]{:S(2)}, u32[]{:S(2)}) collective-permute-start(bf16[128,1536]{1,0:T(8,128)(2,1)} %get-tuple-element.111), channel_id=1, source_target_pairs={{0,4},{4,0},{8,12},{12,8},{16,20},{20,16},{24,28},{28,24},{1,5},{5... | collective-permute-start | bytes 1179656 | tf_op jit(solution)/shard_map/ppermute | solution.py:51
  47.3 38.6 %collective-permute-start.38 = (bf16[128,1536]{1,0:T(8,128)(2,1)}, bf16[128,1536]{1,0:T(8,128)(2,1)S(1)}, u32[]{:S(2)}, u32[]{:S(2)}) collective-permute-start(bf16[128,1536]{1,0:T(8,128)(2,1)} %get-tuple-element.111), channel_id=1, source_target_pairs={{8,0},{12,4},{16,8},{20,12},{24,16},{28,20},{9,1},{13,5},{17,9},{2... | collective-permute-start | bytes 1179656 | tf_op jit(solution)/shard_map/ppermute | solution.py:59
  81.5 42.0 %collective-permute-start = (bf16[256,1536]{1,0:T(8,128)(2,1)S(1)}, bf16[256,1536]{1,0:T(8,128)(2,1)S(1)}, u32[]{:S(2)}, u32[]{:S(2)}) collective-permute-start(bf16[256,1536]{1,0:T(8,128)(2,1)S(1)} %copy-done.57), channel_id=1, source_target_pairs={{0,2},{2,0},{1,3},{3,1},{4,6},{6,4},{5,7},{7,5},{8,10},{10,8},{9,1... | collective-permute-start | bytes 2359304 | tf_op jit(solution)/shard_map/ppermute | solution.py:47
  116.5 43.2 %collective-permute-start.28 = (bf16[192,2048]{1,0:T(8,128)(2,1)S(1)}, bf16[192,2048]{1,0:T(8,128)(2,1)S(1)}, u32[]{:S(2)}, u32[]{:S(2)}) collective-permute-start(bf16[192,2048]{1,0:T(8,128)(2,1)S(1)} %copy-done.40), channel_id=1, source_target_pairs={{8,0},{12,4},{16,8},{20,12},{24,16},{28,20},{9,1},{13,5},{17,9},{2... | collective-permute-start | bytes 2359304 | tf_op jit(solution)/shard_map/ppermute | solution.py:59
  117.8 43.7 %collective-permute-start.29 = (bf16[192,2048]{1,0:T(8,128)(2,1)S(1)}, bf16[192,2048]{1,0:T(8,128)(2,1)S(1)}, u32[]{:S(2)}, u32[]{:S(2)}) collective-permute-start(bf16[192,2048]{1,0:T(8,128)(2,1)S(1)} %copy-done.40), channel_id=1, source_target_pairs={{0,8},{4,12},{8,16},{12,20},{16,24},{20,28},{1,9},{5,13},{9,17},{1... | collective-permute-start | bytes 2359304 | tf_op jit(solution)/shard_map/ppermute | solution.py:55
  158.5 53.5 %collective-permute-start.24 = (bf16[8,48,1536]{2,1,0:T(8,128)(2,1)}, bf16[8,48,1536]{2,1,0:T(8,128)(2,1)S(1)}, u32[]{:S(2)}, u32[]{:S(2)}) collective-permute-start(bf16[8,48,1536]{2,1,0:T(8,128)(2,1)} %bitcast_dynamic-update-slice_fusion.24), channel_id=1, source_target_pairs={{0,1},{1,0},{2,3},{3,2},{4,5},{5,4},{6,7},{7,6},{8,9},{9,8},{10,11... | collective-permute-start | bytes 3538952 | tf_op jit(solution)/shard_map/ppermute | solution.py:43
  176.8 39.7 %collective-permute-start.1 = (bf16[2,256,1536]{2,1,0:T(8,128)(2,1)S(1)}, bf16[2,256,1536]{2,1,0:T(8,128)(2,1)S(1)}, u32[]{:S(2)}, u32[]{:S(2)}) collective-permute-start(bf16[2,256,1536]{2,1,0:T(8,128)(2,1)S(1)} %pad_maximum_fusion.7), channel_id=1, source_target_pairs={{0,1},{1,0},{2,3},{3,2},{4,5},{5,4},{6,7},{7,6},{8,9},{9,8},{10,11... | collective-permute-start | bytes 4718600 | tf_op jit(solution)/shard_map/ppermute | solution.py:43
  208.7 82.8 %collective-permute-start.26 = (bf16[2,256,1536]{2,1,0:T(8,128)(2,1)}, bf16[2,256,1536]{2,1,0:T(8,128)(2,1)}, u32[]{:S(2)}, u32[]{:S(2)}) collective-permute-start(bf16[2,256,1536]{2,1,0:T(8,128)(2,1)} %pad_maximum_fusion.8), channel_id=1, source_target_pairs={{0,1},{1,0},{2,3},{3,2},{4,5},{5,4},{6,7},{7,6},{8,9},{9,8},{10,11... | collective-permute-start | bytes 4718600 | tf_op jit(solution)/shard_map/ppermute | solution.py:43
  209.2 90.6 %collective-permute-start.54 = (bf16[2,256,1536]{2,1,0:T(8,128)(2,1)}, bf16[2,256,1536]{2,1,0:T(8,128)(2,1)}, u32[]{:S(2)}, u32[]{:S(2)}) collective-permute-start(bf16[2,256,1536]{2,1,0:T(8,128)(2,1)} %pad_maximum_fusion.10), channel_id=1, source_target_pairs={{0,1},{1,0},{2,3},{3,2},{4,5},{5,4},{6,7},{7,6},{8,9},{9,8},{10,11... | collective-permute-start | bytes 4718600 | tf_op jit(solution)/shard_map/ppermute | solution.py:43
  216.5 45.3 %collective-permute-start.34 = (bf16[192,2048]{1,0:T(8,128)(2,1)}, bf16[192,2048]{1,0:T(8,128)(2,1)}, u32[]{:S(2)}, u32[]{:S(2)}) collective-permute-start(bf16[192,2048]{1,0:T(8,128)(2,1)} %collective-permute-done.31), channel_id=1, source_target_pairs={{8,0},{12,4},{9,1},{13,5},{10,2},{14,6},{11,3},{15,7}} | collective-permute-start | bytes 2359304 | tf_op jit(solution)/shard_map/ppermute | solution.py:59
  218.7 43.2 %collective-permute-start.35 = (bf16[192,2048]{1,0:T(8,128)(2,1)}, bf16[192,2048]{1,0:T(8,128)(2,1)}, u32[]{:S(2)}, u32[]{:S(2)}) collective-permute-start(bf16[192,2048]{1,0:T(8,128)(2,1)} %collective-permute-done.32), channel_id=1, source_target_pairs={{16,24},{20,28},{17,25},{21,29},{18,26},{22,30},{19,27},{23,31}} | collective-permute-start | bytes 2359304 | tf_op jit(solution)/shard_map/ppermute | solution.py:55
  244.3 51.0 %collective-permute-start.12 = (bf16[4,256,192]{1,2,0:T(8,128)(2,1)}, bf16[4,256,192]{1,2,0:T(8,128)(2,1)}, u32[]{:S(2)}, u32[]{:S(2)}) collective-permute-start(bf16[4,256,192]{1,2,0:T(8,128)(2,1)} %copy.100), channel_id=1, source_target_pairs={{0,2},{2,0},{1,3},{3,1},{4,6},{6,4},{5,7},{7,5},{8,10},{10,8},{9,1... | collective-permute-start | bytes 1179656 | tf_op jit(solution)/shard_map/ppermute | solution.py:47
  455.3 107.7 %collective-permute-start.55 = (bf16[2,256,1536]{2,1,0:T(8,128)(2,1)}, bf16[2,256,1536]{2,1,0:T(8,128)(2,1)S(1)}, u32[]{:S(2)}, u32[]{:S(2)}) collective-permute-start(bf16[2,256,1536]{2,1,0:T(8,128)(2,1)} %bitcast.77), channel_id=1, source_target_pairs={{0,1},{1,0},{2,3},{3,2},{4,5},{5,4},{6,7},{7,6},{8,9},{9,8},{10,11... | collective-permute-start | bytes 4718600 | tf_op jit(solution)/shard_map/ppermute | solution.py:43
  457.2 261.8 %collective-permute-start.88 = (bf16[4,192,2048]{2,1,0:T(8,128)(2,1)}, bf16[4,192,2048]{2,1,0:T(8,128)(2,1)}, u32[]{:S(2)}, u32[]{:S(2)}) collective-permute-start(bf16[4,192,2048]{2,1,0:T(8,128)(2,1)} %dynamic-slice_bitcast_fusion), channel_id=1, source_target_pairs={{0,4},{4,0},{8,12},{12,8},{16,20},{20,16},{24,28},{28,24},{1,5},{5... | collective-permute-start | bytes 9437192 | tf_op jit(solution)/shard_map/ppermute | solution.py:51
  461.3 100.4 %collective-permute-start.97 = (bf16[4,128,1536]{2,1,0:T(8,128)(2,1)S(1)}, bf16[4,128,1536]{2,1,0:T(8,128)(2,1)S(1)}, u32[]{:S(2)}, u32[]{:S(2)}) collective-permute-start(bf16[4,128,1536]{2,1,0:T(8,128)(2,1)S(1)} %dynamic-slice_bitcast_fusion.1), channel_id=1, source_target_pairs={{0,4},{4,0},{8,12},{12,8},{16,20},{20,16},{24,28},{28,24},{1,5},{5... | collective-permute-start | bytes 4718600 | tf_op jit(solution)/shard_map/ppermute | solution.py:51
  463.7 124.0 %collective-permute-start.58 = (bf16[256,1536]{1,0:T(8,128)(2,1)}, bf16[256,1536]{1,0:T(8,128)(2,1)S(1)}, u32[]{:S(2)}, u32[]{:S(2)}) collective-permute-start(bf16[256,1536]{1,0:T(8,128)(2,1)} %fusion.70), channel_id=1, source_target_pairs={{0,2},{2,0},{1,3},{3,1},{4,6},{6,4},{5,7},{7,5},{8,10},{10,8},{9,1... | collective-permute-start | bytes 2359304 | tf_op jit(solution)/shard_map/ppermute | solution.py:47
  465.1 124.8 %collective-permute-start.48 = (bf16[256,1536]{1,0:T(8,128)(2,1)S(1)}, bf16[256,1536]{1,0:T(8,128)(2,1)S(1)}, u32[]{:S(2)}, u32[]{:S(2)}) collective-permute-start(bf16[256,1536]{1,0:T(8,128)(2,1)S(1)} %fusion.76), channel_id=1, source_target_pairs={{0,2},{2,0},{1,3},{3,1},{4,6},{6,4},{5,7},{7,5},{8,10},{10,8},{9,1... | collective-permute-start | bytes 2359304 | tf_op jit(solution)/shard_map/ppermute | solution.py:47
  617.6 119.2 %collective-permute-start.78 = (bf16[8,48,1536]{2,1,0:T(8,128)(2,1)}, bf16[8,48,1536]{2,1,0:T(8,128)(2,1)}, u32[]{:S(2)}, u32[]{:S(2)}) collective-permute-start(bf16[8,48,1536]{2,1,0:T(8,128)(2,1)} %dynamic-slice_bitcast_fusion.2), channel_id=1, source_target_pairs={{0,1},{1,0},{2,3},{3,2},{4,5},{5,4},{6,7},{7,6},{8,9},{9,8},{10,11... | collective-permute-start | bytes 3538952 | tf_op jit(solution)/shard_map/ppermute | solution.py:43
  619.8 94.0 %collective-permute-start.102 = (bf16[128,1536]{1,0:T(8,128)(2,1)}, bf16[128,1536]{1,0:T(8,128)(2,1)}, u32[]{:S(2)}, u32[]{:S(2)}) collective-permute-start(bf16[128,1536]{1,0:T(8,128)(2,1)} %get-tuple-element.161), channel_id=1, source_target_pairs={{24,16},{28,20},{16,8},{20,12},{25,17},{29,21},{17,9},{21,13},{26,... | collective-permute-start | bytes 1179656 | tf_op jit(solution)/shard_map/ppermute | solution.py:59
  621.3 103.4 %collective-permute-start.100 = (bf16[128,1536]{1,0:T(8,128)(2,1)}, bf16[128,1536]{1,0:T(8,128)(2,1)}, u32[]{:S(2)}, u32[]{:S(2)}) collective-permute-start(bf16[128,1536]{1,0:T(8,128)(2,1)} %get-tuple-element.160), channel_id=1, source_target_pairs={{0,8},{4,12},{8,16},{12,20},{16,24},{20,28},{1,9},{5,13},{9,17},{1... | collective-permute-start | bytes 1179656 | tf_op jit(solution)/shard_map/ppermute | solution.py:55
  713.7 69.4 %collective-permute-start.61 = (bf16[2,256,1536]{2,1,0:T(8,128)(2,1)S(1)}, bf16[2,256,1536]{2,1,0:T(8,128)(2,1)S(1)}, u32[]{:S(2)}, u32[]{:S(2)}) collective-permute-start(bf16[2,256,1536]{2,1,0:T(8,128)(2,1)S(1)} %bitcast.524), channel_id=1, source_target_pairs={{0,1},{1,0},{2,3},{3,2},{4,5},{5,4},{6,7},{7,6},{8,9},{9,8},{10,11... | collective-permute-start | bytes 4718600 | tf_op jit(solution)/shard_map/ppermute | solution.py:43
  718.4 65.7 %collective-permute-start.67 = (bf16[2,256,1536]{2,1,0:T(8,128)(2,1)S(1)}, bf16[2,256,1536]{2,1,0:T(8,128)(2,1)S(1)}, u32[]{:S(2)}, u32[]{:S(2)}) collective-permute-start(bf16[2,256,1536]{2,1,0:T(8,128)(2,1)S(1)} %bitcast.523), channel_id=1, source_target_pairs={{0,1},{1,0},{2,3},{3,2},{4,5},{5,4},{6,7},{7,6},{8,9},{9,8},{10,11... | collective-permute-start | bytes 4718600 | tf_op jit(solution)/shard_map/ppermute | solution.py:43
  747.4 103.1 %collective-permute-start.92 = (bf16[192,2048]{1,0:T(8,128)(2,1)S(1)}, bf16[192,2048]{1,0:T(8,128)(2,1)S(1)}, u32[]{:S(2)}, u32[]{:S(2)}) collective-permute-start(bf16[192,2048]{1,0:T(8,128)(2,1)S(1)} %get-tuple-element.145), channel_id=1, source_target_pairs={{24,16},{28,20},{25,17},{29,21},{26,18},{30,22},{27,19},{31,23}} | collective-permute-start | bytes 2359304 | tf_op jit(solution)/shard_map/ppermute | solution.py:59
  778.7 71.9 %collective-permute-start.90 = (bf16[192,2048]{1,0:T(8,128)(2,1)S(1)}, bf16[192,2048]{1,0:T(8,128)(2,1)S(1)}, u32[]{:S(2)}, u32[]{:S(2)}) collective-permute-start(bf16[192,2048]{1,0:T(8,128)(2,1)S(1)} %fusion.58), channel_id=1, source_target_pairs={{0,8},{4,12},{8,16},{12,20},{1,9},{5,13},{9,17},{13,21},{2,10},{6,... | collective-permute-start | bytes 2359304 | tf_op jit(solution)/shard_map/ppermute | solution.py:55
  788.3 35.1 %collective-permute-start.72 = (bf16[192,640]{1,0:T(8,128)(2,1)S(1)}, bf16[192,640]{1,0:T(8,128)(2,1)S(1)}, u32[]{:S(2)}, u32[]{:S(2)}) collective-permute-start(bf16[192,640]{1,0:T(8,128)(2,1)S(1)} %get-tuple-element.172), channel_id=1, source_target_pairs={{0,8},{4,12},{8,16},{12,20},{16,24},{20,28},{1,9},{5,13},{9,17},{1... | collective-permute-start | bytes 737288 | tf_op jit(solution)/shard_map/ppermute | solution.py:55
  817.6 45.2 %collective-permute-start.62 = (bf16[256,1536]{1,0:T(8,128)(2,1)S(1)}, bf16[256,1536]{1,0:T(8,128)(2,1)S(1)}, u32[]{:S(2)}, u32[]{:S(2)}) collective-permute-start(bf16[256,1536]{1,0:T(8,128)(2,1)S(1)} %fusion.67), channel_id=1, source_target_pairs={{0,2},{2,0},{1,3},{3,1},{4,6},{6,4},{5,7},{7,5},{8,10},{10,8},{9,1... | collective-permute-start | bytes 2359304 | tf_op jit(solution)/shard_map/ppermute | solution.py:47
  823.4 39.4 %collective-permute-start.68 = (bf16[256,1536]{1,0:T(8,128)(2,1)S(1)}, bf16[256,1536]{1,0:T(8,128)(2,1)S(1)}, u32[]{:S(2)}, u32[]{:S(2)}) collective-permute-start(bf16[256,1536]{1,0:T(8,128)(2,1)S(1)} %fusion.62), channel_id=1, source_target_pairs={{0,2},{2,0},{1,3},{3,1},{4,6},{6,4},{5,7},{7,5},{8,10},{10,8},{9,1... | collective-permute-start | bytes 2359304 | tf_op jit(solution)/shard_map/ppermute | solution.py:47
  860.0 54.1 %collective-permute-start.77 = (bf16[2,192,640]{2,1,0:T(8,128)(2,1)S(1)}, bf16[2,192,640]{2,1,0:T(8,128)(2,1)S(1)}, u32[]{:S(2)}, u32[]{:S(2)}) collective-permute-start(bf16[2,192,640]{2,1,0:T(8,128)(2,1)S(1)} %pad_maximum_fusion.22), channel_id=1, source_target_pairs={{0,1},{1,0},{2,3},{3,2},{4,5},{5,4},{6,7},{7,6},{8,9},{9,8},{10,11... | collective-permute-start | bytes 1474568 | tf_op jit(solution)/shard_map/ppermute | solution.py:43
  (165 other events, 2517.2 us)

commit v2 on v1

v2 whole, which is shorter than its diff:
```python
import functools

import jax
import jax.numpy as jnp
from jax import lax
from jax.experimental import pallas as pl
from jax.experimental.pallas import tpu as pltpu
from jax.sharding import PartitionSpec as P

epsilon = 1e-06
gelu_scale = 0.7978845608028654
gelu_cubic = 0.044715
low = jnp.bfloat16
wide = jnp.float32
lanes = 128


def rms_forward(features):
    inverse = lax.rsqrt(jnp.mean(features * features, axis=-1, keepdims=True) + epsilon)
    return (features * inverse, inverse)


def rms_backward(upstream, normed, inverse, gain):
    scaled = upstream * gain
    return inverse * (scaled - normed * jnp.mean(scaled * normed, axis=-1, keepdims=True))


def gelu_pair(gate_pre):
    inner_argument = gelu_scale * (gate_pre + gelu_cubic * gate_pre * gate_pre * gate_pre)
    tanh_part = jnp.tanh(inner_argument)
    gelu_value = 0.5 * gate_pre * (1.0 + tanh_part)
    gelu_slope = 0.5 * (1.0 + tanh_part) + 0.5 * gate_pre * (
        1.0 - tanh_part * tanh_part
    ) * gelu_scale * (1.0 + 3.0 * gelu_cubic * gate_pre * gate_pre)
    return (gelu_value, gelu_slope)


def mm(left, right, dims, out=low):
    return lax.dot_general(left, right, ((dims[:1], dims[1:]), ((), ())), preferred_element_type=wide).astype(out)


def flip_core(array):
    return lax.ppermute(array, "seq", [(0, 1), (1, 0), (2, 3), (3, 2)])


def flip_y(array):
    return lax.ppermute(array, "seq", [(0, 2), (2, 0), (1, 3), (3, 1)])


class Later:
    value = None


class Rounds:
    def __init__(self):
        self.jobs, self.ended = [], ()

    def add(self, job, *operands, open_end=False):
        self.jobs.append((job, operands, open_end, Later()))
        return self.jobs[-1][3]

    def close(self):
        given = []
        for job, operands, open_end, later in self.jobs:
            given.append([o.value if isinstance(o, Later) else o for o in operands])
        given, unused = lax.optimization_barrier((given, self.ended))
        ended = []
        for (job, operands, open_end, later), arrays in zip(self.jobs, given):
            later.value = job(*arrays)
            if not open_end:
                ended.append(later.value)
        self.jobs, self.ended = [], ended


def flip_x(array):
    return lax.ppermute(array, "dp", [(d, d ^ 1) for d in range(8)])


def turn_z(array):
    return lax.ppermute(array, "dp", [(d, (d + 2) % 8) for d in range(8)])


def by_ring():
    return lax.axis_size("dp") == 8


def owner_order():
    d = lax.axis_index("dp")
    z, x = d // 2, d % 2
    return jnp.stack([2 * ((z - r) % 4) + (x if side == 0 else 1 - x) for r in range(4) for side in (0, 1)])


def ring_blocks(parts):
    d = lax.axis_index("dp")
    z, x = d // 2, d % 2
    pick = lambda index: lax.dynamic_index_in_dim(parts, index, 0, keepdims=False)
    order = [2 * ((z - 1 - r) % 4) for r in range(4)]
    return [pick(at + x) for at in order], [pick(at + 1 - x) for at in order]


def joined(*arrays):
    return sum(array.astype(wide) for array in arrays).astype(low)


def sum_dp(small):
    size = lax.axis_size("dp")
    step = 1
    while step < size:
        small = small + lax.ppermute(small, "dp", [(d, d ^ step) for d in range(size)])
        step *= 2
    return small


def by_slot(groups, s):
    grid = groups.reshape((2, 2) + groups.shape[1:])
    grid = jnp.swapaxes(grid, 0, 1)
    grid = jnp.where(s % 2 == 1, grid[::-1], grid)
    grid = jnp.where(s // 2 == 1, grid[:, ::-1], grid)
    return grid.reshape(groups.shape)


def by_index(slots, s):
    grid = slots.reshape((2, 2) + slots.shape[1:])
    grid = jnp.where(s % 2 == 1, grid[::-1], grid)
    grid = jnp.where(s // 2 == 1, grid[:, ::-1], grid)
    return jnp.swapaxes(grid, 0, 1).reshape(slots.shape)


def half_of(per):
    return -(-(-(-per // 4)) // 16) * 8


def pick_kernel(s_ref, gate_ref, up_ref, down_ref, *out_refs, owners, per, half):
    model = down_ref.shape[1]
    third = model // 3
    for choice in range(4):

        @pl.when(s_ref[0] == choice)
        def _():
            for part, out_ref in enumerate(out_refs):
                offset = (2 * choice + part) * half
                width = max(0, min(half, per - offset))
                for side, ref in enumerate((gate_ref, up_ref)):
                    pieces = []
                    for d in range(owners):
                        start = d * per + offset
                        pieces.append(ref[:, start : start + width])
                        if width < half:
                            pieces.append(jnp.zeros((ref.shape[0], half - width), ref.dtype))
                    out_ref[:, side * owners * half : (side + 1) * owners * half] = jnp.concatenate(pieces, axis=1)
                rows = down_ref[offset : offset + width, :]
                if width < half:
                    rows = jnp.concatenate([rows, jnp.zeros((half - width, model), rows.dtype)], axis=0)
                for j in range(3):
                    out_ref[j * half : (j + 1) * half, 2 * owners * half :] = rows[:, j * third : (j + 1) * third]


def pick_units(gate, up, down, s):
    owners = lax.axis_size("dp")
    rows, total = gate.shape
    per, model = down.shape
    half = half_of(per)
    if not by_ring():
        halves = []
        for part in range(2):
            start = (2 * s + part) * half
            sides = []
            for weight in (gate, up):
                padded = jnp.pad(weight.reshape(rows, owners, per), ((0, 0), (0, 0), (0, 8 * half - per)))
                sides.append(lax.dynamic_slice_in_dim(padded, start, half, 2).reshape(rows, owners * half))
            padded = jnp.pad(down, ((0, 8 * half - per), (0, 0)))
            block = lax.dynamic_slice_in_dim(padded, start, half, 0).reshape(half, 3, model // 3)
            sides.append(jnp.swapaxes(block, 0, 1).reshape(3 * half, model // 3))
            halves.append(jnp.concatenate(sides, axis=1))
        return halves
    return pl.pallas_call(
        functools.partial(pick_kernel, owners=owners, per=per, half=half),
        out_shape=[jax.ShapeDtypeStruct((rows, model), gate.dtype)] * 2,
        grid_spec=pltpu.PrefetchScalarGridSpec(
            num_scalar_prefetch=1,
            grid=(1,),
            in_specs=[pl.BlockSpec(w.shape, lambda i, s: (0, 0)) for w in (gate, up, down)],
            out_specs=[pl.BlockSpec((rows, model), lambda i, s: (0, 0))] * 2,
        ),
        name="pick_units",
    )(s.reshape(1), gate, up, down)


def place_kernel(first_ref, second_ref, gate_ref, up_ref, down_ref, *, owners, per, half):
    refs = (first_ref, second_ref)
    model = down_ref.shape[1]
    third = model // 3
    spans = []
    for choice in range(4):
        for part in range(2):
            offset = (2 * choice + part) * half
            spans.append((choice, part, offset, max(0, min(half, per - offset))))
    for side, ref in enumerate((gate_ref, up_ref)):
        for d in range(owners):
            pieces = []
            for choice, part, offset, width in spans:
                at = (side * owners + d) * half
                pieces.append(refs[part][choice, :, at : at + width].astype(wide))
            ref[:, d * per : (d + 1) * per] = jnp.concatenate(pieces, axis=1)
    for choice, part, offset, width in spans:
        for j in range(3):
            down_ref[offset : offset + width, j * third : (j + 1) * third] = refs[part][
                choice, j * half : j * half + width, 2 * owners * half :
            ].astype(wide)


def place_units(halves, per):
    owners = lax.axis_size("dp")
    rows, model = halves[0].shape[1:]
    half = half_of(per)
    total = per * owners
    if not by_ring():
        outs = []
        for side in range(2):
            at = side * owners * half
            grid = jnp.stack([h[:, :, at : at + owners * half].reshape(4, rows, owners, half) for h in halves], axis=3)
            flat = grid.transpose(1, 2, 0, 3, 4).reshape(rows, owners, 8 * half)[:, :, :per]
            outs.append(flat.reshape(rows, total).astype(wide))
        grid = jnp.stack([h[:, :, 2 * owners * half :].reshape(4, 3, half, model // 3) for h in halves], axis=1)
        outs.append(grid.transpose(0, 1, 3, 2, 4).reshape(8 * half, model)[:per].astype(wide))
        return outs
    return pl.pallas_call(
        functools.partial(place_kernel, owners=owners, per=per, half=half),
        out_shape=[
            jax.ShapeDtypeStruct((rows, total), wide),
            jax.ShapeDtypeStruct((rows, total), wide),
            jax.ShapeDtypeStruct((per, model), wide),
        ],
        name="place_units",
    )(*halves)


def load_blocks(place_ref, block_refs, moves, sems):
    copies = []
    for k, ref in enumerate(block_refs):
        for source, target in moves(ref, place_ref[k]):
            copies.append(pltpu.make_async_copy(source, target, sems.at[len(copies)]))
    for copy in copies:
        copy.start()
    for copy in copies:
        copy.wait()


def rows_at(index, size):
    return pl.ds(pl.multiple_of(index * size, size), size)


def project_kernel(place_ref, *refs, ring, inner, slots):
    token_refs, refs = refs[:4], refs[4:]
    count = 8 if ring else 1
    block_refs, refs = refs[:count], refs[count:]
    qkv_ref, normed_ref, weight_ref, gain_ref, taken = refs[:5]
    step = pl.program_id(0)

    @pl.when(step == 0)
    def _():
        if ring:
            rows = block_refs[0].shape[0]
            load_blocks(
                place_ref, block_refs, lambda ref, owner: [(ref, weight_ref.at[rows_at(owner, rows), :])], refs[5]
            )
        else:
            weight_ref[...] = block_refs[0][...]
        base = 3 * inner // lanes * lanes
        turned = weight_ref[:, base : base + lanes].astype(wide).T
        gain_ref[...] = turned[3 * inner - base : 3 * inner - base + 8]

    for slot in range(4):

        @pl.when(step % slots == slot)
        def _():
            taken[...] = token_refs[slot][0]

    features = taken[...].astype(wide)
    inverse = lax.rsqrt(jnp.mean(features * features, axis=-1, keepdims=True) + epsilon)
    normed = (features * inverse * gain_ref[0:1, :]).astype(low)
    normed_ref[...] = normed
    columns = 3 * inner
    qkv_ref[...] = jnp.dot(normed, weight_ref[:, :columns], preferred_element_type=wide).astype(low)


def project_heads(tokens, blocks, order, inner):
    micro_count, rows, model = tokens[0].shape
    ring = by_ring()
    columns = blocks[0].shape[1]
    total = micro_count * 4 * rows
    whole = pl.BlockSpec((model, columns), lambda i, p: (0, 0))
    return pl.pallas_call(
        functools.partial(project_kernel, ring=ring, inner=inner, slots=4),
        out_shape=[
            jax.ShapeDtypeStruct((total, 3 * inner), low),
            jax.ShapeDtypeStruct((total, model), low),
            jax.ShapeDtypeStruct((model, columns), low),
            jax.ShapeDtypeStruct((8, model), wide),
        ],
        grid_spec=pltpu.PrefetchScalarGridSpec(
            num_scalar_prefetch=1,
            grid=(micro_count * 4,),
            in_specs=[pl.BlockSpec((1, rows, model), lambda i, p: (i // 4, 0, 0))] * 4
            + ([pl.BlockSpec(memory_space=pl.ANY)] * 8 if ring else [whole]),
            out_specs=[
                pl.BlockSpec((rows, 3 * inner), lambda i, p: (i, 0)),
                pl.BlockSpec((rows, model), lambda i, p: (i, 0)),
                whole,
                pl.BlockSpec((8, model), lambda i, p: (0, 0)),
            ],
            scratch_shapes=[pltpu.VMEM((rows, model), low)] + ([pltpu.SemaphoreType.DMA((8,))] if ring else []),
        ),
        cost_estimate=pl.CostEstimate(
            flops=6 * total * model * inner, transcendentals=0, bytes_accessed=4 * total * model + 2 * model * columns
        ),
        name="project_heads",
    )(order, *tokens, *blocks)


def mix_kernel(*refs, slots):
    token_refs, part_refs = refs[:4], refs[4:8]
    mix_ref, gain_ref = refs[8:10]
    ffn_ref, middle_ref, attended_ref, taken = refs[-4:]
    step = pl.program_id(0)
    for slot in range(4):

        @pl.when(step == slot)
        def _():
            taken[...] = token_refs[slot][0]

    attended = jnp.concatenate([ref[...] for ref in part_refs], axis=1)
    middle = taken[...].astype(wide) + jnp.dot(attended, mix_ref[...], preferred_element_type=wide)
    inverse = lax.rsqrt(jnp.mean(middle * middle, axis=-1, keepdims=True) + epsilon)
    ffn_ref[...] = (middle * inverse * gain_ref[1:2, :]).astype(low)

    @pl.when(step == 0)
    def _():
        middle_ref[...] = middle
        attended_ref[...] = attended


def mix_heads(tokens, parts, mix, gains, micro, before):
    micro_count, rows, model = tokens[0].shape
    inner = parts[0].shape[1]
    own = lambda i: (0, 0)
    swaps = (0, 1, 2, 3)
    return pl.pallas_call(
        functools.partial(mix_kernel, slots=4),
        out_shape=[
            jax.ShapeDtypeStruct((micro_count * 4 * rows, model), low),
            jax.ShapeDtypeStruct((rows, model), wide),
            jax.ShapeDtypeStruct((rows, 4 * inner), low),
        ],
        grid=(4,),
        in_specs=[pl.BlockSpec((1, rows, model), lambda i: (micro, 0, 0))] * 4
        + [pl.BlockSpec((rows, inner), lambda i, k=k: (i ^ k, 0)) for k in swaps]
        + [pl.BlockSpec(mix.shape, own), pl.BlockSpec(gains.shape, own)]
        + ([] if before is None else [pl.BlockSpec(memory_space=pl.ANY)]),
        out_specs=[
            pl.BlockSpec((rows, model), lambda i: (i + 4 * micro, 0)),
            pl.BlockSpec((rows, model), own),
            pl.BlockSpec((rows, 4 * inner), own),
        ],
        scratch_shapes=[pltpu.VMEM((rows, model), low)],
        input_output_aliases={} if before is None else {10: 0},
        cost_estimate=pl.CostEstimate(
            flops=32 * rows * model * inner, transcendentals=0, bytes_accessed=24 * rows * model
        ),
        name="mix_heads",
    )(*tokens, *parts, mix, gains, *([] if before is None else [before]))


def slot_index(slot, s):
    return s ^ (2 * (slot % 2) + slot // 2)


def toeplitz_kernel(offsets_ref, out_ref, *, block, heads):
    for head in range(heads):
        row = jnp.broadcast_to(offsets_ref[head : head + 1, :], (block, offsets_ref.shape[1]))
        width = row.shape[1]
        rolled = pltpu.roll(row, width - block, 1, stride=1, stride_axis=0)
        out_ref[head] = rolled[:, : width - block]


def toeplitz(per_offset, block):
    heads, width = per_offset.shape
    return pl.pallas_call(
        functools.partial(toeplitz_kernel, block=block, heads=heads),
        out_shape=jax.ShapeDtypeStruct((heads, block, width - block), wide),
        name="toeplitz",
    )(per_offset)


def forward_kernel(s_ref, rows_ref, all_ref, bias_ref, out_ref, probs_ref, *, heads, size, block):
    s = s_ref[0]
    here = slot_index(pl.program_id(0), s)
    inner = heads * size
    outs = []
    for head in range(heads):
        query = rows_ref[:, head * size : (head + 1) * size]
        key = all_ref[:, inner + head * size : inner + (head + 1) * size]
        value = all_ref[:, 2 * inner + head * size : 2 * inner + (head + 1) * size]
        scores = lax.dot_general(query, key, (((1,), (1,)), ((), ())), preferred_element_type=wide)
        pieces = []
        for slot in range(4):
            start = pl.multiple_of((slot_index(slot, s) - here + 3) * block, block)
            pieces.append(scores[:, slot * block : (slot + 1) * block] + bias_ref[head, :, pl.ds(start, block)])
        scores = jnp.concatenate(pieces, axis=1)
        expo = jnp.exp(scores - jnp.max(scores, axis=-1, keepdims=True))
        probs = (expo * (1.0 / jnp.sum(expo, axis=-1, keepdims=True))).astype(low)
        probs_ref[head] = probs
        outs.append(jnp.dot(probs, value, preferred_element_type=wide))
    out_ref[...] = jnp.concatenate(outs, axis=1).astype(low)


def attend_forward(mixed, bias, s, heads, micro, length):
    columns = mixed.shape[1]
    inner = columns // 3
    block = length // 4
    return pl.pallas_call(
        functools.partial(forward_kernel, heads=heads, size=inner // heads, block=block),
        out_shape=[
            jax.ShapeDtypeStruct((length, inner), low),
            jax.ShapeDtypeStruct((heads, length, length), low),
        ],
        grid_spec=pltpu.PrefetchScalarGridSpec(
            num_scalar_prefetch=1,
            grid=(4,),
            in_specs=[
                pl.BlockSpec((block, columns), lambda i, s: (i + 4 * micro, 0)),
                pl.BlockSpec((length, columns), lambda i, s: (micro, 0)),
                pl.BlockSpec(bias.shape, lambda i, s: (0, 0, 0)),
            ],
            out_specs=[
                pl.BlockSpec((block, inner), lambda i, s: (i, 0)),
                pl.BlockSpec((heads, block, length), lambda i, s: (0, i, 0)),
            ],
        ),
        cost_estimate=pl.CostEstimate(
            flops=16 * length * length * inner, transcendentals=heads * length * length,
            bytes_accessed=2 * heads * length * length + bias.size * 4,
        ),
        name="attend_forward",
    )(s.reshape(1), mixed, mixed, bias)


def backward_kernel(
    s_ref, rows_ref, all_ref, grad_ref, probs_ref, out_ref, sums_ref, key_ref, value_ref, *, heads, size, block
):
    s = s_ref[0]
    step = pl.program_id(0)
    here = slot_index(step, s)
    inner = heads * size

    @pl.when(step == 0)
    def _():
        sums_ref[...] = jnp.zeros_like(sums_ref)
        key_ref[...] = jnp.zeros_like(key_ref)
        value_ref[...] = jnp.zeros_like(value_ref)

    outs = []
    for head in range(heads):
        query = rows_ref[:, head * size : (head + 1) * size]
        key = all_ref[:, inner + head * size : inner + (head + 1) * size]
        value = all_ref[:, 2 * inner + head * size : 2 * inner + (head + 1) * size]
        grad = grad_ref[:, head * size : (head + 1) * size]
        probs_low = probs_ref[head]
        probs = probs_low.astype(wide)
        prob_grad = lax.dot_general(grad, value, (((1,), (1,)), ((), ())), preferred_element_type=wide)
        centred = jnp.sum(probs * prob_grad, axis=-1, keepdims=True)
        score_low = (probs * (prob_grad - centred)).astype(low)
        outs.append(jnp.dot(score_low, key, preferred_element_type=wide))
        key_ref[head] += lax.dot_general(query, score_low, (((0,), (0,)), ((), ())), preferred_element_type=wide)
        value_ref[head] += lax.dot_general(grad, probs_low, (((0,), (0,)), ((), ())), preferred_element_type=wide)
        for slot in range(4):
            start = pl.multiple_of((slot_index(slot, s) - here + 3) * block, block)
            sums_ref[head, :, pl.ds(start, block)] += score_low[:, slot * block : (slot + 1) * block].astype(wide)
    at = pl.multiple_of(step * block, block)
    out_ref[pl.ds(at, block), :inner] = jnp.concatenate(outs, axis=1).astype(low)

    @pl.when(step == 3)
    def _():
        turned = [key_ref[head].T for head in range(heads)] + [value_ref[head].T for head in range(heads)]
        out_ref[:, inner:] = jnp.concatenate(turned, axis=1).astype(low)


def attend_backward(mixed, grad, probs, s, heads, micro):
    columns = mixed.shape[1]
    length = probs.shape[1]
    inner = columns // 3
    block = length // 4
    size = inner // heads
    return pl.pallas_call(
        functools.partial(backward_kernel, heads=heads, size=size, block=block),
        out_shape=[
            jax.ShapeDtypeStruct((length, columns), low),
            jax.ShapeDtypeStruct((heads, block, 2 * length - block), wide),
        ],
        grid_spec=pltpu.PrefetchScalarGridSpec(
            num_scalar_prefetch=1,
            grid=(4,),
            in_specs=[
                pl.BlockSpec((block, columns), lambda i, s: (i + 4 * micro, 0)),
                pl.BlockSpec((length, columns), lambda i, s: (micro, 0)),
                pl.BlockSpec((block, inner), lambda i, s: (i, 0)),
                pl.BlockSpec((heads, block, length), lambda i, s: (0, i, 0)),
            ],
            out_specs=[
                pl.BlockSpec((length, columns), lambda i, s: (0, 0)),
                pl.BlockSpec((heads, block, 2 * length - block), lambda i, s: (0, 0, 0)),
            ],
            scratch_shapes=[pltpu.VMEM((heads, size, length), wide), pltpu.VMEM((heads, size, length), wide)],
        ),
        cost_estimate=pl.CostEstimate(
            flops=32 * length * length * inner, transcendentals=0,
            bytes_accessed=2 * heads * length * length + heads * block * length * 8,
        ),
        name="attend_backward",
    )(s.reshape(1), mixed, mixed, grad, probs)


def diagonal_kernel(*refs, heads, block):
    out_ref = refs[-1]
    width = refs[0].shape[2] + block
    for head in range(heads):
        total = refs[0][head]
        for ref in refs[1:-1]:
            total = total + ref[head]
        total = jnp.concatenate([total, jnp.zeros((block, block), wide)], axis=1)
        rows = block
        while rows > 8:
            rows //= 2
            total = total[:rows] + pltpu.roll(total[rows:], width - rows, 1)
        total = pltpu.roll(total, block, 1)
        line = total[0:1]
        for row in range(1, 8):
            line = line + pltpu.roll(total[row : row + 1], width - row, 1)
        out_ref[head : head + 1, :] = line


def diagonal_sums(sums):
    heads, block, width = sums[0].shape
    return pl.pallas_call(
        functools.partial(diagonal_kernel, heads=heads, block=block),
        out_shape=jax.ShapeDtypeStruct((heads, width + block), wide),
        name="diagonal_sums",
    )(*sums)


def ffn_kernel(place_ref, *refs, ring, first, width):
    x_ref, refs = refs[0], refs[1:]
    g_count = 4 if first else 1
    g_refs, refs = refs[:g_count], refs[g_count:]
    count = 8 if ring else 2
    block_refs, refs = refs[:count], refs[count:]
    step = pl.program_id(0)
    slot = step % 4
    if first:
        hidden_ref, grads_ref, result_ref, back_ref, all_g_ref, refs = *refs[:5], refs[5:]
    else:
        result_before, back_before, refs = *refs[:2], refs[2:]
        refs = refs[-(6 + (3 if ring else 0)) :]
        hidden_ref, grads_ref, near_result, far_result, near_back, far_back, refs = *refs[:6], refs[6:]
    if ring:
        sides_ref, down_ref, sems = refs[-3:]
        rows = block_refs[0].shape[0]
        half = rows // 3

        @pl.when(step == 0)
        def _():
            def moves(ref, owner):
                pieces = [(ref.at[:, : 2 * width], sides_ref.at[rows_at(owner, rows), :])]
                for j in range(3):
                    pieces.append(
                        (ref.at[j * half : (j + 1) * half, 2 * width :], down_ref.at[j, rows_at(owner, half), :])
                    )
                return pieces

            load_blocks(place_ref, block_refs, moves, sems)
    else:
        sides_ref, down_ref = block_refs
    third = down_ref.shape[2]
    if first:
        for k in range(4):

            @pl.when(slot == k)
            def _():
                all_g_ref[...] = g_refs[k][0]

        g_ref = all_g_ref
    else:
        g_ref = g_refs[0]
    x = x_ref[...]
    tile = min(256, width)
    for start in range(0, width, tile):
        gate_pre = jnp.dot(x, sides_ref[:, start : start + tile], preferred_element_type=wide)
        up_pre = jnp.dot(x, sides_ref[:, width + start : width + start + tile], preferred_element_type=wide)
        hidden_grad = 0.0
        for j in range(3):
            hidden_grad = hidden_grad + lax.dot_general(
                g_ref[:, j * third : (j + 1) * third],
                down_ref[j, start : start + tile, :],
                (((1,), (1,)), ((), ())),
                preferred_element_type=wide,
            )
        gelu_value, gelu_slope = gelu_pair(gate_pre)
        hidden_ref[:, start : start + tile] = (gelu_value * up_pre).astype(low)
        grads_ref[:, start : start + tile] = (hidden_grad * up_pre * gelu_slope).astype(low)
        grads_ref[:, width + start : width + start + tile] = (hidden_grad * gelu_value).astype(low)
    hidden = hidden_ref[...]
    grads = grads_ref[...]
    for j in range(3):
        span = slice(j * third, (j + 1) * third)
        back = lax.dot_general(grads, sides_ref[span, :], (((1,), (1,)), ((), ())), preferred_element_type=wide)
        result = jnp.dot(hidden, down_ref[j], preferred_element_type=wide)
        if first:
            back_ref[:, span] = back.astype(low)
            result_ref[:, span] = result.astype(low)
        else:
            back = (back + back_before[:, span].astype(wide)).astype(low)
            result = (result + result_before[:, span].astype(wide)).astype(low)

            @pl.when(slot < 2)
            def _():
                near_back[:, span] = back
                near_result[:, span] = result

            @pl.when(slot >= 2)
            def _():
                far_back[:, span] = back
                far_result[:, span] = result


def ffn_weights(blocks, model, ring, width):
    if ring:
        return blocks, [pl.BlockSpec(memory_space=pl.ANY)] * 8
    whole = blocks[0]
    owners = lax.axis_size("dp")
    half = width // owners
    down = whole[:, 2 * width :].reshape(owners, 3, half, model // 3)
    down = jnp.swapaxes(down, 0, 1).reshape(3, width, model // 3)
    sides = whole[:, : 2 * width]
    return [sides, down], [
        pl.BlockSpec(sides.shape, lambda i, p: (0, 0)),
        pl.BlockSpec(down.shape, lambda i, p: (0, 0, 0)),
    ]


def ffn_scratch(ring, model, width):
    if not ring:
        return []
    return [
        pltpu.VMEM((model, 2 * width), low),
        pltpu.VMEM((3, width, model // 3), low),
        pltpu.SemaphoreType.DMA((32,)),
    ]


def ffn_cost(tokens, model, width):
    return pl.CostEstimate(
        flops=12 * tokens * model * width,
        transcendentals=tokens * width,
        bytes_accessed=8 * tokens * model + 6 * tokens * width + 6 * model * width,
    )


def ffn_first(x, g_slots, blocks, order):
    tokens, model = x.shape
    micro_count, rows = g_slots[0].shape[:2]
    width = model // 3
    ring = by_ring()
    weights, specs = ffn_weights(blocks, model, ring, width)
    row = lambda i, p: (i, 0)
    return pl.pallas_call(
        functools.partial(ffn_kernel, ring=ring, first=True, width=width),
        out_shape=[
            jax.ShapeDtypeStruct((tokens, width), low),
            jax.ShapeDtypeStruct((tokens, 2 * width), low),
            jax.ShapeDtypeStruct((tokens, model), low),
            jax.ShapeDtypeStruct((tokens, model), low),
            jax.ShapeDtypeStruct((tokens, model), low),
        ],
        grid_spec=pltpu.PrefetchScalarGridSpec(
            num_scalar_prefetch=1,
            grid=(tokens // rows,),
            in_specs=[pl.BlockSpec((rows, model), row)]
            + [pl.BlockSpec((1, rows, model), lambda i, p: (i // 4, 0, 0))] * 4
            + specs,
            out_specs=[
                pl.BlockSpec((rows, width), row),
                pl.BlockSpec((rows, 2 * width), row),
                pl.BlockSpec((rows, model), row),
                pl.BlockSpec((rows, model), row),
                pl.BlockSpec((rows, model), row),
            ],
            scratch_shapes=ffn_scratch(ring, model, width),
        ),
        cost_estimate=ffn_cost(tokens, model, width),
        name="ffn_first",
    )(order, x, *g_slots, *weights)


def ffn_second(x, g, blocks, order, result, back, micro, rows, before):
    tokens, model = x.shape
    width = model // 3
    ring = by_ring()
    weights, specs = ffn_weights(blocks, model, ring, width)
    row = lambda i, p: (i + 4 * micro, 0)
    near = pl.BlockSpec((rows, model), lambda i, p: (jnp.minimum(i, 1), 0))
    far = pl.BlockSpec((rows, model), lambda i, p: (jnp.maximum(i - 2, 0), 0))
    at = 1 + 2 + len(weights) + 2
    return pl.pallas_call(
        functools.partial(ffn_kernel, ring=ring, first=False, width=width),
        out_shape=[jax.ShapeDtypeStruct((tokens, width), low), jax.ShapeDtypeStruct((tokens, 2 * width), low)]
        + [jax.ShapeDtypeStruct((2 * rows, model), low)] * 4,
        grid_spec=pltpu.PrefetchScalarGridSpec(
            num_scalar_prefetch=1,
            grid=(4,),
            in_specs=[pl.BlockSpec((rows, model), row)] * 2
            + specs
            + [pl.BlockSpec((rows, model), row)] * 2
            + ([] if before is None else [pl.BlockSpec(memory_space=pl.ANY)] * 2),
            out_specs=[pl.BlockSpec((rows, width), row), pl.BlockSpec((rows, 2 * width), row), near, far, near, far],
            scratch_shapes=ffn_scratch(ring, model, width),
        ),
        input_output_aliases={} if before is None else {at: 0, at + 1: 1},
        cost_estimate=ffn_cost(4 * rows, model, width),
        name="ffn_second",
    )(order, x, g, *weights, result, back, *([] if before is None else before))


def back_kernel(grad_ref, weight_ref, near_ref, far_ref):
    step = pl.program_id(0)
    columns = grad_ref.shape[1]
    out = lax.dot_general(
        grad_ref[...], weight_ref[:, :columns], (((1,), (1,)), ((), ())), preferred_element_type=wide
    ).astype(low)

    @pl.when(step < 2)
    def _():
        near_ref[...] = out

    @pl.when(step >= 2)
    def _():
        far_ref[...] = out


def heads_back(grad, weights):
    total, columns = grad.shape
    model = weights.shape[0]
    rows = total // 4
    return pl.pallas_call(
        back_kernel,
        out_shape=[jax.ShapeDtypeStruct((2 * rows, model), low)] * 2,
        grid=(4,),
        in_specs=[pl.BlockSpec((rows, columns), lambda i: (i, 0)), pl.BlockSpec(weights.shape, lambda i: (0, 0))],
        out_specs=[
            pl.BlockSpec((rows, model), lambda i: (jnp.minimum(i, 1), 0)),
            pl.BlockSpec((rows, model), lambda i: (jnp.maximum(i - 2, 0), 0)),
        ],
        cost_estimate=pl.CostEstimate(
            flops=2 * total * columns * model, transcendentals=0, bytes_accessed=2 * total * model + 2 * model * columns
        ),
        name="heads_back",
    )(grad, weights)


def per_device(
    tokens,
    query_weight,
    key_weight,
    value_weight,
    mix_weight,
    gate_weight,
    up_weight,
    down_weight,
    attn_gain,
    ffn_gain,
    bias_table,
    bucket_ids,
    out_grad,
):
    owners = lax.axis_size("dp")
    s = lax.axis_index("seq")
    core = s % 2
    micro_count = tokens.shape[0]
    local, model = tokens.shape[2:]
    bucket_count, heads = bias_table.shape
    length = bucket_ids.shape[0] // 2
    per = down_weight.shape[0]
    half = half_of(per)
    width = owners * half
    inner = query_weight.shape[1] // 4
    mix_rows = mix_weight.shape[0] // 2
    shard_rows = query_weight.shape[0]
    ring = by_ring()

    own_heads = [lax.dynamic_slice_in_dim(w, s * inner, inner, 1) for w in (query_weight, key_weight, value_weight)]
    gain_columns = jnp.pad(jnp.stack([attn_gain, ffn_gain], axis=1), ((0, 0), (0, 62)))
    mix_part = lax.dynamic_slice_in_dim(mix_weight, core * mix_rows, mix_rows, 0)
    mix_columns = jnp.swapaxes(mix_part.reshape(mix_rows, 4, model // 4), 0, 1).reshape(shard_rows, model // 4)
    head_shard = jnp.concatenate(own_heads + [gain_columns, mix_columns], axis=1)

    onehot = (jnp.arange(bucket_count, dtype=jnp.int32)[:, None] == bucket_ids[None, :]).astype(wide)
    per_offset = lax.dot_general(
        bias_table, onehot, (((0,), (0,)), ((), ())), precision=lax.Precision.HIGHEST
    )
    own_tokens, own_grad = tokens[:, 0], out_grad[:, 0]
    order = owner_order() if ring else jnp.arange(8)
    rounds = Rounds()
    add, close = rounds.add, rounds.close
    gathered = lambda shard: [lax.all_gather(shard, "dp", axis=0, tiled=True)]

    token_y = add(flip_y, own_tokens, open_end=True)
    token_core = add(flip_core, own_tokens)
    units = add(lambda *w: pick_units(*w, s), gate_weight, up_weight, down_weight)
    bias = add(lambda p: toeplitz(p, local), per_offset)
    heads_z, heads_x, first_z, first_x, second_z, second_x = ([] for unused in range(6))

    def along(shard, held, crossed, turn, cross):
        if not held:
            held.append(shard)
        if ring and turn:
            held.append(add(turn_z, held[-1]))
        if ring and cross is not None:
            crossed.append(add(flip_x, held[cross]))

    def value_of(item):
        return item.value if isinstance(item, Later) else item

    def blocks_of(shard, held, crossed):
        if not ring:
            return gathered(value_of(shard))
        return [value_of(item) for pair in zip(held, crossed) for item in pair]

    heads_at = lambda turn, cross: along(head_shard, heads_z, heads_x, turn, cross)
    first_at = lambda turn, cross: along(units.value[0], first_z, first_x, turn, cross)
    second_at = lambda turn, cross: along(units.value[1], second_z, second_x, turn, cross)
    heads_at(True, 0)
    close()
    heads_at(True, 1)
    close()
    heads_at(True, 2)
    close()
    heads_at(False, 3)
    first_at(True, None)
    token_both = add(flip_core, token_y)
    grad_y = add(flip_y, own_grad, open_end=True)
    grad_core = add(flip_core, own_grad)
    close()
    token_slots = [own_tokens, token_y.value, token_core.value, token_both.value]
    projected = add(
        lambda *a: project_heads(a[:4], a[4:], order, inner),
        *token_slots,
        *blocks_of(head_shard, heads_z, heads_x),
    )
    first_at(True, 0)
    close()
    qkv, normed, head_weights, gains = projected.value
    forward = [add(lambda q, b: attend_forward(q, b, s, heads, 0, length), qkv, bias)]
    mix_half = head_weights[:, 3 * inner + 64 :]
    mix_other = add(flip_core, mix_half)
    first_at(True, 1)
    close()
    part_y, part_core, part_both = [], [], []
    for micro in range(1, micro_count):
        forward.append(add(lambda q, b, m=micro: attend_forward(q, b, s, heads, m, length), qkv, bias))
        part_y.append(add(flip_y, forward[micro - 1].value[0]))
        part_core.append(add(flip_core, forward[micro - 1].value[0]))
        if micro == 1:
            first_at(False, 2)
            second_at(True, None)
        close()
    attended = [item.value[0] for item in forward]

    def ordered_mix(mine, other):
        halves = [m.reshape(owners, 4, mix_rows, model // 4) for m in (mine, other)]
        full_mix = jnp.stack(
            [jnp.where(core == 0, halves[0], halves[1]), jnp.where(core == 0, halves[1], halves[0])], axis=1
        )
        full_mix = full_mix.transpose(0, 1, 3, 2, 4).reshape(4, inner, model)
        return by_slot(full_mix, s).reshape(4 * inner, model)

    slot_mix = add(ordered_mix, mix_half, mix_other)
    part_y.append(add(flip_y, attended[-1]))
    part_core.append(add(flip_core, attended[-1]))
    for item in part_y[:-1]:
        part_both.append(add(flip_core, item))
    grad_both = add(flip_core, grad_y)
    first_at(False, 3)
    second_at(True, None)
    close()
    slot_mix = slot_mix.value
    grad_slots = [own_grad, grad_y.value, grad_core.value, grad_both.value]
    ffn_low = None
    saved = []
    for micro in range(micro_count):
        sources = token_slots + [attended[micro], part_y[micro].value, part_core[micro].value, part_both[micro].value]
        given = [] if ffn_low is None else [ffn_low]
        mixed = add(
            lambda *a, m=micro: mix_heads(a[:4], a[4:8], a[8], a[9], m, a[10] if m else None),
            *sources, slot_mix, gains, *given,
        )
        if micro == 0:
            part_both.append(add(flip_core, part_y[-1]))
            second_at(True, 0)
        if micro == 1:
            second_at(False, 1)
        close()
        ffn_low, middle, attended_own = mixed.value
        saved.append((forward[micro].value[1], middle, attended_own))

    first_half = add(
        lambda *a: ffn_first(a[0], a[1:5], a[5:], order),
        ffn_low, *grad_slots, *blocks_of(units.value[0], first_z, first_x),
    )
    second_at(False, 2)
    second_at(False, 3)
    close()
    first_hidden, first_grads, result, back, all_g = first_half.value
    second_blocks = blocks_of(units.value[1], second_z, second_x)

    def unit_grads(x, g, hidden, grads):
        sides = mm(x, grads, (0, 0)).reshape(owners, shard_rows, 2 * width)
        down = mm(hidden, g, (0, 0)).reshape(owners, half, 3, model // 3)
        down = jnp.swapaxes(down, 1, 2).reshape(owners, shard_rows, model // 3)
        parts = jnp.concatenate([sides, down], axis=2)
        return ring_blocks(parts) if ring else parts

    class Scatter:
        def __init__(self, parts):
            self.crossed, self.turned = [], []
            self.parts = parts
            if not ring:
                self.total = lax.psum_scatter(parts, "dp", scatter_dimension=0, tiled=False)

        def cross(self):
            if ring:
                self.crossed.append(add(flip_x, self.parts[1][len(self.crossed)]))

        def block(self, step):
            arrays = [self.parts[0][step], self.crossed[step].value]
            return arrays + ([self.turned[step - 1].value] if step else [])

        def turn(self):
            if ring:
                self.turned.append(add(lambda *a: turn_z(joined(*a)), *self.block(len(self.turned))))

        def sum(self):
            return joined(*self.block(3)) if ring else self.total.astype(low)

    first_parts = add(unit_grads, ffn_low, all_g, first_hidden, first_grads)
    close()
    first_sum = Scatter(first_parts.value)
    second, sums, arrived_back, arrived_result, away_back = None, [], [], [], []
    for micro in range(micro_count):
        given = [] if second is None else second
        outs = add(
            lambda *a, m=micro: ffn_second(
                a[0], a[1], a[2 : 2 + len(second_blocks)], order, *a[2 + len(second_blocks) : 4 + len(second_blocks)],
                m, local, list(a[4 + len(second_blocks) :]) if m else None,
            ),
            ffn_low, all_g, *second_blocks, result, back, *given,
        )
        first_sum.cross()
        if micro == 1:
            first_sum.turn()
            arrived_back.append(add(flip_core, sums[0][3]))
        close()
        second = list(outs.value[:2])
        sums.append([part.reshape(2, local, model) for part in outs.value[2:]])

    def away(near, arrived):
        return flip_y(joined(near[1], arrived[1]))

    def own_sum(near, arrived, last):
        return near[0].astype(wide) + arrived[0].astype(wide) + last.astype(wide)

    second_parts = add(unit_grads, ffn_low, all_g, *second)
    away_back.append(add(away, sums[0][2], arrived_back[0]))
    arrived_back.append(add(flip_core, sums[1][3]))
    for micro in range(micro_count):
        arrived_result.append(add(flip_core, sums[micro][1]))
    first_sum.cross()
    first_sum.turn()
    close()

    gain_one, gain_two = gains[0], gains[1]

    def after_ffn(near, arrived, last, middle, own, gain, mix):
        ffn_in = own_sum(near, arrived, last)
        normed_middle, inverse_middle = rms_forward(middle)
        middle_grad = own.astype(wide) + rms_backward(ffn_in, normed_middle, inverse_middle, gain)
        mix_in = middle_grad.astype(low)
        attended_grad = mm(mix_in, mix, (1, 1))
        parts = [attended_grad[:, k * inner : (k + 1) * inner] for k in range(4)]
        return middle_grad, mix_in, parts[0], jnp.stack([parts[1], parts[3]]), parts[2]

    def after_at(micro):
        return add(
            after_ffn, sums[micro][2], arrived_back[micro], away_back[micro], saved[micro][1], own_grad[micro],
            gain_two, slot_mix,
        )

    second_sum = Scatter(second_parts.value)
    after = [after_at(0)]
    away_back.append(add(away, sums[1][2], arrived_back[1]))
    first_sum.cross()
    first_sum.turn()
    close()
    after.append(after_at(1))
    far, near_own, near_far = [], [], []
    far.append(add(flip_y, after[0].value[3]))
    near_own.append(add(flip_core, after[0].value[4]))
    first_total = add(lambda: first_sum.sum())
    second_sum.cross()
    close()
    far.append(add(flip_y, after[1].value[3]))
    near_own.append(add(flip_core, after[1].value[4]))
    near_far.append(add(flip_core, far[0].value[1]))
    second_sum.cross()
    second_sum.turn()

    def mix_grads(*arrays):
        left, right = jnp.concatenate(arrays[:micro_count]), jnp.concatenate(arrays[micro_count:])
        grad_mix = by_index(mm(left, right, (0, 0)).reshape(4, inner, model), s).reshape(owners, 2, mix_rows, model)
        kept = lax.dynamic_index_in_dim(grad_mix, core, 1, keepdims=False)
        return kept, lax.dynamic_index_in_dim(grad_mix, 1 - core, 1, keepdims=False)

    mix_pair = add(mix_grads, *[item[2] for item in saved], *[item.value[1] for item in after])
    close()
    backward, away_result = [], []

    def attend_at(micro):
        blocks = [after[micro].value[2], far[micro].value[0], near_own[micro].value, near_far[micro].value]
        return add(
            lambda q, p, *b: attend_backward(q, jnp.concatenate(b), p, s, heads, micro), qkv, saved[micro][0], *blocks
        )

    backward.append(attend_at(0))
    near_far.append(add(flip_core, far[1].value[1]))
    away_result.append(add(away, sums[0][0], arrived_result[0]))
    mix_arrived = add(flip_core, mix_pair.value[1])
    second_sum.cross()
    second_sum.turn()
    close()
    backward.append(attend_at(1))
    away_result.append(add(away, sums[1][0], arrived_result[1]))
    mix_parts = add(lambda a, b: ring_blocks(joined(a, b)) if ring else joined(a, b), mix_pair.value[0], mix_arrived)
    second_sum.cross()
    second_sum.turn()
    close()
    mix_scatter = Scatter(mix_parts.value)
    outputs = [
        (saved[micro][1] + own_sum(sums[micro][0], arrived_result[micro].value, away_result[micro].value)).astype(low)
        for micro in range(micro_count)
    ]
    qkv_grads = [item.value[0] for item in backward]
    diagonals = [item.value[1] for item in backward]
    unit_slots = []

    def own_and_y(total):
        return [total, add(flip_y, total), add(flip_core, total)]

    unit_slots.append(own_and_y(first_total.value))
    returned = [add(heads_back, grad, head_weights) for grad in qkv_grads]
    second_total = add(lambda: second_sum.sum())
    for unused in range(4):
        mix_scatter.cross()
    close()
    unit_slots.append(own_and_y(second_total.value))
    halves = [[part.reshape(2, local, model) for part in item.value] for item in returned]
    arrived_in = [add(flip_core, far_part) for near_part, far_part in halves]

    def head_grads(x, *grads):
        parts = mm(x, jnp.concatenate(grads), (0, 0)).reshape(owners, shard_rows, 3 * inner)
        return ring_blocks(parts) if ring else parts

    head_parts = add(head_grads, normed, *qkv_grads)
    unit_slots[0].append(add(flip_core, unit_slots[0][1].value))
    mix_scatter.turn()
    close()
    head_scatter = Scatter(head_parts.value)
    away_in = [add(away, halves[0][0], arrived_in[0])]
    for unused in range(4):
        head_scatter.cross()
    unit_slots[1].append(add(flip_core, unit_slots[1][1].value))
    mix_scatter.turn()
    diagonal = add(lambda *d: diagonal_sums(d), *diagonals)
    close()
    away_in.append(add(away, halves[1][0], arrived_in[1]))
    head_scatter.turn()
    mix_scatter.turn()

    def stacked(slots):
        return by_index(jnp.stack([value_of(item) for item in slots]), s)

    placed = add(lambda a, b: place_units([a, b], per), stacked(unit_slots[0]), stacked(unit_slots[1]))
    close()
    head_scatter.turn()
    mix_total = mix_scatter.sum()
    mix_y = add(flip_y, mix_total)
    close()
    mix_sum = joined(mix_total, mix_y.value)
    mix_two = add(flip_core, mix_sum)
    head_scatter.turn()
    table_local = lax.dot_general(
        onehot, diagonal.value, (((1,), (1,)), ((), ())), precision=lax.Precision.HIGHEST
    )
    grad_bias_table = sum_dp(table_local)
    input_grads = []
    for micro in range(micro_count):
        attn_in = own_sum(halves[micro][0], arrived_in[micro].value, away_in[micro].value)
        normed_own, inverse_own = rms_forward(own_tokens[micro].astype(wide))
        input_grads.append(after[micro].value[0] + rms_backward(attn_in, normed_own, inverse_own, gain_one))
    close()
    head_total = head_scatter.sum()
    head_y = flip_y(head_total)
    head_slots = [head_total, head_y, flip_core(head_total), flip_core(head_y)]
    mix_two = mix_two.value
    grad_mix = jnp.concatenate(
        [jnp.where(core == 0, mix_sum, mix_two), jnp.where(core == 0, mix_two, mix_sum)]
    ).astype(wide)
    grad_gate, grad_up, grad_down = placed.value
    head_parts = stacked(head_slots).astype(wide)
    grad_query, grad_key, grad_value = (
        jnp.concatenate([head_parts[i, :, k * inner : (k + 1) * inner] for i in range(4)], axis=1) for k in range(3)
    )

    def gain_grad(gain, pairs):
        return sum(jnp.sum(weight.astype(wide) * grad, axis=1) for weight, grad in pairs) / gain.astype(wide)

    grad_attn_gain = gain_grad(
        attn_gain, ((query_weight, grad_query), (key_weight, grad_key), (value_weight, grad_value))
    )
    grad_ffn_gain = gain_grad(ffn_gain, ((gate_weight, grad_gate), (up_weight, grad_up)))
    return (
        jnp.stack(outputs)[:, None],
        jnp.stack(input_grads)[:, None],
        grad_query,
        grad_key,
        grad_value,
        grad_mix,
        grad_gate,
        grad_up,
        grad_down,
        grad_attn_gain,
        grad_ffn_gain,
        grad_bias_table,
    )


def solution(mesh):
    in_specs = (
        P(None, "dp", "seq", None),
        P("dp", None),
        P("dp", None),
        P("dp", None),
        P("dp", None),
        P("dp", None),
        P("dp", None),
        P("dp", None),
        P("dp"),
        P("dp"),
        P(None, "seq"),
        P(),
        P(None, "dp", "seq", None),
    )
    out_specs = (
        P(None, "dp", "seq", None),
        P(None, "dp", "seq", None),
        P("dp", None),
        P("dp", None),
        P("dp", None),
        P("dp", None),
        P("dp", None),
        P("dp", None),
        P("dp", None),
        P("dp"),
        P("dp"),
        P(None, "seq"),
    )
    return jax.shard_map(
        per_device, mesh=mesh, in_specs=in_specs, out_specs=out_specs, check_vma=False
    )
```

time: 939 us -> 627 us (0.67)
  waiting for transfers between devices: 337 us -> 169 us
  starting transfers between devices: 179 us -> 74.8 us
  Pallas kernels: 109 us -> 198 us
  matrix products: 114 us -> 45.3 us
  local copies, waits for them, and re-layouts: 96.7 us -> 47.6 us
    ppermute x48 -> x21, starting transfers between devices: 127 us -> 13.9 us  [turn_z(): return lax.ppermute(array, 'dp', [(d, (d + 2) % 8) for d in range(8)])]
    ppermute x20 -> x28, waiting for transfers between devices: 159 us -> 48 us  [flip_x(): return lax.ppermute(array, 'dp', [(d, d ^ 1) for d in range(8)])]
    pallas_call x4 -> x10, Pallas kernels: 40.1 us -> 130 us  [the longest x2 40.5 us: ffn_second(): pl.pallas_call(functools.partial(ffn_kernel, ring=ring, first=False, widt...]
    dot_general x16 -> x8, matrix products: 113 us -> 43.5 us  [mm(): lax.dot_general(left, right, ((dims[:1], dims[1:]), ((), ())), preferred_...]
    ppermute x48 -> x21, waiting for transfers between devices: 101 us -> 55.3 us  [turn_z(): return lax.ppermute(array, 'dp', [(d, (d + 2) % 8) for d in range(8)])]
    dynamic_update_slice x19 -> x0, local copies, waits for them, and re-layouts: 16.7 us -> none  [gather_dp(): lax.dynamic_update_slice(whole, block[None], (2 * at + across, 0, 0))]
    gather x8 -> x0, local copies, waits for them, and re-layouts: 16.2 us -> none  [the longest x4 8.62 us: per_device(): from_y = flip_y(blocks)[jnp.array([1, 0, 3, 2])]]
    slice x15 -> x4, local copies, waits for them, and re-layouts: 17.9 us -> 2.71 us  [the longest x1 1.51 us: per_device(): mix_half = head_weights[:, 3 * inner + 64:]]
  transfers between devices with their start and end apart: 109 -> 95, of which waited for: 33 -> 36; matrix products, arithmetic and copies ran while one was open for 22% -> 18% of each run, Pallas kernels for 8% -> 30%
where the time goes in v2:
time: 627 us; the launch traced here: 619 us
  Pallas kernels  198 us (32%)
  waiting for transfers between devices  169 us (27%)
  other arithmetic  81.5 us (13%)
  starting transfers between devices  74.8 us (12%)
  local copies, waits for them, and re-layouts  47.6 us (8%)
  matrix products  45.3 us (7%)
    ppermute x16, waiting for transfers between devices, flip_y(): return lax.ppermute(array, 'seq', [(0, 2), (2, 0), (1, 3), (3, 1)])  63.4 us
    ppermute x21, waiting for transfers between devices, turn_z(): return lax.ppermute(array, 'dp', [(d, (d + 2) % 8) for d in range(8)])  55.3 us
    ppermute x28, waiting for transfers between devices, flip_x(): return lax.ppermute(array, 'dp', [(d, d ^ 1) for d in range(8)])  48 us
    dot_general x8, matrix products, mm(): lax.dot_general(left, right, ((dims[:1], dims[1:]), ((), ())), preferred_...  43.5 us
    pallas_call x2, Pallas kernels, ffn_second(): pl.pallas_call(functools.partial(ffn_kernel, ring=ring, first=False, widt...  40.5 us
    pallas_call x2, Pallas kernels, attend_backward(): pl.pallas_call(functools.partial(backward_kernel, heads=heads, size=size,...  31.9 us
    ppermute x28, starting transfers between devices, flip_x(): return lax.ppermute(array, 'dp', [(d, d ^ 1) for d in range(8)])  30 us
    pallas_call x1, Pallas kernels, ffn_first(): pl.pallas_call(functools.partial(ffn_kernel, ring=ring, first=True, width...  29.7 us
  transfers between devices with their start and end apart: 95, of which 36 were waited for; matrix products, arithmetic and copies ran while one was open for 18% of the time, Pallas kernels for 30%

profile of v2, /device:TPU:0, one launch (start us, length us, event | category | flops | bytes accessed | tf_op | source)
XLA Modules:
  0.0 619.2 jit_solution(4288787249916020848)
XLA Ops:
  26.0 10.1 %collective-permute-done.4.refs_8_ = bf16[192,1024]{1,0:T(8,128)(2,1)S(1)} collective-permute-done((bf16[192,1024]{1,0:T(8,128)(2,1)}, bf16[192,1024]{1,0:T(8,128)(2,1)S(1)}, u32[]{:S(2)}, u32[]{:S(2)}) %collective-permute-start.4) | collective-permute-done | bytes 393248 | tf_op jit(solution)/shard_map/ppermute | solution.py:80
  37.7 7.5 %collective-permute-done.refs_1_ = bf16[2,256,1536]{2,1,0:T(8,128)(2,1)} collective-permute-done((bf16[2,256,1536]{2,1,0:T(8,128)(2,1)S(1)}, bf16[2,256,1536]{2,1,0:T(8,128)(2,1)}, u32[]{:S(2)}, u32[]{:S(2)}) %collective-permute-start) | collective-permute-done | bytes 1572896 | tf_op jit(solution)/shard_map/ppermute | solution.py:47
  50.3 9.5 %collective-permute-done.9.refs_11_ = bf16[192,1024]{1,0:T(8,128)(2,1)S(1)} collective-permute-done((bf16[192,1024]{1,0:T(8,128)(2,1)S(1)}, bf16[192,1024]{1,0:T(8,128)(2,1)S(1)}, u32[]{:S(2)}, u32[]{:S(2)}) %collective-permute-start.9) | collective-permute-done | bytes 393248 | tf_op jit(solution)/shard_map/ppermute | solution.py:76
  59.8 6.3 %collective-permute-done.10.refs_7_ = bf16[192,1536]{1,0:T(8,128)(2,1)} collective-permute-done((bf16[192,1536]{1,0:T(8,128)(2,1)}, bf16[192,1536]{1,0:T(8,128)(2,1)}, u32[]{:S(2)}, u32[]{:S(2)}) %collective-permute-start.10) | collective-permute-done | bytes 589856 | tf_op jit(solution)/shard_map/ppermute | solution.py:80
  69.5 15.5 %project_heads.1 = (bf16[2048,576]{1,0:T(8,128)(2,1)}, bf16[2048,1536]{1,0:T(8,128)(2,1)}, bf16[1536,1024]{1,0:T(8,128)(2,1)}, f32[8,1536]{1,0:T(8,128)}) custom-call(s32[8]{0:T(128)} %stack.133.place_ref, bf16[2,256,1536]{2,1,0:T(8,128)(2,1)} %bitcast.275, bf16[2,256,1536]{2,1,0:T(8,128)(2,1)} %collective-permute-done.refs_1_, ...), custom_call_target="tpu_custom_call" | custom-call | flops 3623878656 | bytes 15728640 | tf_op jit(solution)/shard_map/project_heads/pallas_call | solution.py:293
  88.4 12.8 %attend_forward.2 = (bf16[1024,192]{1,0:T(8,128)(2,1)}, bf16[3,1024,1024]{2,1,0:T(8,128)(2,1)}) custom-call(s32[1]{0:T(128)} %bitcast.4.s_ref, bf16[2048,576]{1,0:T(8,128)(2,1)} %get-tuple-element.526.rows_ref.all_ref, bf16[2048,576]{1,0:T(8,128)(2,1)} %get-tuple-element.526.rows_ref.all_ref, f32[3,256,1792]{2,1,0:T(8,128)} %toeplitz.1.bias_ref), custom_call_target="tpu_custom_call" | custom-call | flops 3221225472 | bytes 11796480 | tf_op jit(solution)/shard_map/attend_forward/pallas_call | solution.py:421
  107.6 12.9 %attend_forward.3 = (bf16[1024,192]{1,0:T(8,128)(2,1)}, bf16[3,1024,1024]{2,1,0:T(8,128)(2,1)}) custom-call(s32[1]{0:T(128)} %bitcast.4.s_ref, bf16[2048,576]{1,0:T(8,128)(2,1)} %get-tuple-element.526.rows_ref.all_ref, bf16[2048,576]{1,0:T(8,128)(2,1)} %get-tuple-element.526.rows_ref.all_ref, f32[3,256,1792]{2,1,0:T(8,128)} %toeplitz.1.bias_ref), custom_call_target="tpu_custom_call" | custom-call | flops 3221225472 | bytes 11796480 | tf_op jit(solution)/shard_map/attend_forward/pallas_call | solution.py:421
  124.2 10.7 %collective-permute-done.17.refs_5_ = bf16[1024,192]{1,0:T(8,128)(2,1)} collective-permute-done((bf16[1024,192]{1,0:T(8,128)(2,1)}, bf16[1024,192]{1,0:T(8,128)(2,1)}, u32[]{:S(2)}, u32[]{:S(2)}) %collective-permute-start.17) | collective-permute-done | bytes 393248 | tf_op jit(solution)/shard_map/ppermute | solution.py:47
  150.4 9.3 %collective-permute-done.23.refs_5_ = bf16[1024,192]{1,0:T(8,128)(2,1)} collective-permute-done((bf16[1024,192]{1,0:T(8,128)(2,1)S(1)}, bf16[1024,192]{1,0:T(8,128)(2,1)}, u32[]{:S(2)}, u32[]{:S(2)}) %collective-permute-start.23) | collective-permute-done | bytes 393248 | tf_op jit(solution)/shard_map/ppermute | solution.py:47
  163.5 9.4 %mix_heads.2 = (bf16[2048,1536]{1,0:T(8,128)(2,1)}, f32[256,1536]{1,0:T(8,128)}, bf16[256,768]{1,0:T(8,128)(2,1)}) custom-call(bf16[2,256,1536]{2,1,0:T(8,128)(2,1)} %bitcast.276, bf16[2,256,1536]{2,1,0:T(8,128)(2,1)} %collective-permute-done.refs_1_, bf16[2,256,1536]{2,1,0:T(8,128)(2,1)} %copy-done.10, bf16[2,256,1536]{2,1,0:T(8,128)(2,1)} %copy-done.11, ...), custom_call_target="tpu_custom_call" | custom-call | flops 2415919104 | bytes 9437184 | tf_op jit(solution)/shard_map/mix_heads/pallas_call | solution.py:348
  172.9 7.1 %collective-permute-done.29.refs_8_ = bf16[192,1536]{1,0:T(8,128)(2,1)S(1)} collective-permute-done((bf16[192,1536]{1,0:T(8,128)(2,1)}, bf16[192,1536]{1,0:T(8,128)(2,1)S(1)}, u32[]{:S(2)}, u32[]{:S(2)}) %collective-permute-start.29) | collective-permute-done | bytes 589856 | tf_op jit(solution)/shard_map/ppermute | solution.py:80
  183.0 9.4 %mix_heads.3 = (bf16[2048,1536]{1,0:T(8,128)(2,1)}, f32[256,1536]{1,0:T(8,128)}, bf16[256,768]{1,0:T(8,128)(2,1)}) custom-call(bf16[2,256,1536]{2,1,0:T(8,128)(2,1)} %bitcast.277, bf16[2,256,1536]{2,1,0:T(8,128)(2,1)} %collective-permute-done.refs_1_, bf16[2,256,1536]{2,1,0:T(8,128)(2,1)} %copy-done.10, ...), custom_call_target="tpu_custom_call", output_to_operand_aliasing={{0}: (10, {})} | custom-call | flops 2415919104 | bytes 9437184 | tf_op jit(solution)/shard_map/mix_heads/pallas_call | solution.py:348
  197.4 29.7 %ffn_first.1 = (bf16[2048,512]{1,0:T(8,128)(2,1)}, bf16[2048,1024]{1,0:T(8,128)(2,1)}, bf16[2048,1536]{1,0:T(8,128)(2,1)}, bf16[2048,1536]{1,0:T(8,128)(2,1)}, bf16[2048,1536]{1,0:T(8,128)(2,1)}) custom-call(s32[8]{0:T(128)} %stack.133.place_ref, bf16[2048,1536]{1,0:T(8,128)(2,1)} %get-tuple-element.470.refs_0_, bf16[2,256,1536]{2,1,0:T(8,128)(2,1)} %bitcast.319, ...), custom_call_target="tpu_custom_call" | custom-call | flops 19327352832 | bytes 36175872 | tf_op jit(solution)/shard_map/ffn_first/pallas_call | solution.py:675
  228.1 8.0 %convolution_convert_fusion.5 = bf16[512,1536]{1,0:T(8,128)(2,1)} fusion(bf16[2048,512]{1,0:T(8,128)(2,1)} %get-tuple-element.417, bf16[2048,1536]{1,0:T(8,128)(2,1)} %get-tuple-element.473.refs_1_), kind=kOutput, calls=%fused_computation.48 | convolution fusion | flops 3222011904 | bytes 9961472 | tf_op jit(solution)/shard_map/dot_general | solution.py:39
  241.1 10.3 %convolution_convert_fusion.1 = bf16[1536,1024]{1,0:T(8,128)(2,1)S(1)} fusion(bf16[2048,1536]{1,0:T(8,128)(2,1)} %get-tuple-element.470.refs_0_, bf16[2048,1024]{1,0:T(8,128)(2,1)} %get-tuple-element.416), kind=kOutput, calls=%fused_computation.33 | convolution fusion | flops 6444023808 | bytes 13631488 | tf_op jit(solution)/shard_map/dot_general | solution.py:39
  254.6 20.2 %ffn_second.2 = (bf16[2048,512]{1,0:T(8,128)(2,1)}, bf16[2048,1024]{1,0:T(8,128)(2,1)}, bf16[512,1536]{1,0:T(8,128)(2,1)}, bf16[512,1536]{1,0:T(8,128)(2,1)}, bf...) custom-call(s32[8]{0:T(128)} %stack.133.place_ref, bf16[2048,1536]{1,0:T(8,128)(2,1)} %get-tuple-element.470.refs_0_, ...), custom_call_target="tpu_custom_call" | custom-call | flops 9663676416 | bytes 20447232 | tf_op jit(solution)/shard_map/ffn_second/pallas_call | solution.py:713
  280.1 20.3 %ffn_second.3 = (bf16[2048,512]{1,0:T(8,128)(2,1)}, bf16[2048,1024]{1,0:T(8,128)(2,1)}, bf16[512,1536]{1,0:T(8,128)(2,1)}, bf16[512,1536]{1,0:T(8,128)(2,1)}, bf...) custom-call(s32[8]{0:T(128)} %stack.133.place_ref, ...), custom_call_target="tpu_custom_call", output_to_operand_aliasing={{0}: (13, {}), {1}: (14, {})} | custom-call | flops 9663676416 | bytes 20447232 | tf_op jit(solution)/shard_map/ffn_second/pallas_call | solution.py:713
  306.7 9.2 %convolution_convert_fusion = bf16[1536,1024]{1,0:T(8,128)(2,1)S(1)} fusion(bf16[2048,1536]{1,0:T(8,128)(2,1)} %get-tuple-element.470.refs_0_, bf16[2048,1024]{1,0:T(8,128)(2,1)S(1)} %copy-done.15), kind=kOutput, calls=%fused_computation.32 | convolution fusion | flops 6444023808 | bytes 13631488 | tf_op jit(solution)/shard_map/dot_general | solution.py:39
  331.8 12.3 %collective-permute-done.41 = bf16[192,1536]{1,0:T(8,128)(2,1)S(1)} collective-permute-done((bf16[192,1536]{1,0:T(8,128)(2,1)S(1)}, bf16[192,1536]{1,0:T(8,128)(2,1)S(1)}, u32[]{:S(2)}, u32[]{:S(2)}) %collective-permute-start.41) | collective-permute-done | bytes 589856 | tf_op jit(solution)/shard_map/ppermute | solution.py:76
  356.2 6.2 collective-permute-done.46
  363.4 5.9 collective-permute-done.44
  411.0 16.0 %attend_backward.2 = (bf16[1024,576]{1,0:T(8,128)(2,1)}, f32[3,256,1792]{2,1,0:T(8,128)}) custom-call(s32[1]{0:T(128)} %bitcast.4.s_ref, bf16[2048,576]{1,0:T(8,128)(2,1)} %get-tuple-element.526.rows_ref.all_ref, bf16[2048,576]{1,0:T(8,128)(2,1)} %get-tuple-element.526.rows_ref.all_ref, bf16[1024,192]{1,0:T(8,128)(2,1)} %pad_maximum_fusion.6.grad_ref, ...), custom_call_target="tpu_custom_call" | custom-call | flops 6442450944 | bytes 12582912 | tf_op jit(solution)/shard_map/attend_backward/pallas_call | solution.py:494
  438.4 15.9 %attend_backward.3 = (bf16[1024,576]{1,0:T(8,128)(2,1)}, f32[3,256,1792]{2,1,0:T(8,128)}) custom-call(s32[1]{0:T(128)} %bitcast.4.s_ref, bf16[2048,576]{1,0:T(8,128)(2,1)} %get-tuple-element.526.rows_ref.all_ref, bf16[2048,576]{1,0:T(8,128)(2,1)} %get-tuple-element.526.rows_ref.all_ref, bf16[1024,192]{1,0:T(8,128)(2,1)} %pad_maximum_fusion.7.grad_ref, ...), custom_call_target="tpu_custom_call" | custom-call | flops 6442450944 | bytes 12582912 | tf_op jit(solution)/shard_map/attend_backward/pallas_call | solution.py:494
  466.5 7.1 %heads_back.3 = (bf16[512,1536]{1,0:T(8,128)(2,1)}, bf16[512,1536]{1,0:T(8,128)(2,1)}) custom-call(bf16[1024,576]{1,0:T(8,128)(2,1)} %get-tuple-element.557.grad_ref, bf16[1536,1024]{1,0:T(8,128)(2,1)} %get-tuple-element.545.weight_ref), custom_call_target="tpu_custom_call" | custom-call | flops 1811939328 | bytes 4915200 | tf_op jit(solution)/shard_map/heads_back/pallas_call | solution.py:753
  474.5 7.1 %heads_back.2 = (bf16[512,1536]{1,0:T(8,128)(2,1)}, bf16[512,1536]{1,0:T(8,128)(2,1)}) custom-call(bf16[1024,576]{1,0:T(8,128)(2,1)} %get-tuple-element.556.grad_ref, bf16[1536,1024]{1,0:T(8,128)(2,1)} %get-tuple-element.545.weight_ref), custom_call_target="tpu_custom_call" | custom-call | flops 1811939328 | bytes 4915200 | tf_op jit(solution)/shard_map/heads_back/pallas_call | solution.py:753
  484.5 8.3 %convolution_convert_fusion.3 = bf16[1536,576]{0,1:T(8,128)(2,1)} fusion(bf16[2048,1536]{1,0:T(8,128)(2,1)} %get-tuple-element.555, bf16[1024,576]{1,0:T(8,128)(2,1)} %get-tuple-element.557.grad_ref, bf16[1024,576]{1,0:T(8,128)(2,1)S(1)} %copy-done.91), kind=kOutput, calls=%fused_computation.44 | convolution fusion | flops 3629481984 | bytes 10420224 | tf_op jit(solution)/shard_map/dot_general | solution.py:39
  499.8 11.5 %collective-permute-done.70 = bf16[192,1536]{1,0:T(8,128)(2,1)S(1)} collective-permute-done((bf16[192,1536]{1,0:T(8,128)(2,1)S(1)}, bf16[192,1536]{1,0:T(8,128)(2,1)S(1)}, u32[]{:S(2)}, u32[]{:S(2)}) %collective-permute-start.70) | collective-permute-done | bytes 589856 | tf_op jit(solution)/shard_map/ppermute | solution.py:47
  513.0 6.5 %diagonal_sums.1 = f32[3,2048]{1,0:T(4,128)} custom-call(f32[3,256,1792]{2,1,0:T(8,128)} %get-tuple-element.574.refs_0_, f32[3,256,1792]{2,1,0:T(8,128)} %get-tuple-element.575.refs_1_), custom_call_target="tpu_custom_call" | custom-call | tf_op jit(solution)/shard_map/diagonal_sums/pallas_call | solution.py:544
  555.5 7.5 %place_units.1 = (f32[192,3968]{1,0:T(8,128)}, f32[192,3968]{1,0:T(8,128)}, f32[496,1536]{1,0:T(8,128)}) custom-call(bf16[4,192,1536]{2,1,0:T(8,128)(2,1)} %bitcast.294, bf16[4,192,1536]{2,1,0:T(8,128)(2,1)} %bitcast.295), custom_call_target="tpu_custom_call" | custom-call | tf_op jit(solution)/shard_map/place_units/pallas_call | solution.py:227
  575.3 6.3 %collective-permute-done.84 = bf16[192,576]{1,0:T(8,128)(2,1)S(1)} collective-permute-done((bf16[192,576]{1,0:T(8,128)(2,1)S(1)}, bf16[192,576]{1,0:T(8,128)(2,1)S(1)}, u32[]{:S(2)}, u32[]{:S(2)}) %collective-permute-start.84) | collective-permute-done | bytes 221216 | tf_op jit(solution)/shard_map/ppermute | solution.py:80
  581.6 7.6 %collective-permute-done.82 = bf16[256,1536]{1,0:T(8,128)(2,1)S(1)} collective-permute-done((bf16[256,1536]{1,0:T(8,128)(2,1)S(1)}, bf16[256,1536]{1,0:T(8,128)(2,1)S(1)}, u32[]{:S(2)}, u32[]{:S(2)}) %collective-permute-start.82) | collective-permute-done | bytes 786464 | tf_op jit(solution)/shard_map/ppermute | solution.py:47
  599.4 6.1 collective-permute-done.87
  (488 shorter events, 274.1 us)
Async XLA Ops:
  7.5 37.7 %collective-permute-start = (bf16[2,256,1536]{2,1,0:T(8,128)(2,1)S(1)}, bf16[2,256,1536]{2,1,0:T(8,128)(2,1)}, u32[]{:S(2)}, u32[]{:S(2)}) collective-permute-start(bf16[2,256,1536]{2,1,0:T(8,128)(2,1)S(1)} %bitcast.279), channel_id=1, source_target_pairs={{0,2},{2,0},{1,3},{3,1},{4,6},{6,4},{5,7},{7,5},{8,10},{10,8},{9,1... | collective-permute-start | bytes 4718600 | tf_op jit(solution)/shard_map/ppermute | solution.py:47
  86.8 37.3 %collective-permute-start.19 = (bf16[2,256,1536]{2,1,0:T(8,128)(2,1)S(1)}, bf16[2,256,1536]{2,1,0:T(8,128)(2,1)}, u32[]{:S(2)}, u32[]{:S(2)}) collective-permute-start(bf16[2,256,1536]{2,1,0:T(8,128)(2,1)S(1)} %bitcast.320), channel_id=1, source_target_pairs={{0,2},{2,0},{1,3},{3,1},{4,6},{6,4},{5,7},{7,5},{8,10},{10,8},{9,1... | collective-permute-start | bytes 4718600 | tf_op jit(solution)/shard_map/ppermute | solution.py:47
  105.0 29.9 %collective-permute-start.20 = (bf16[192,1536]{1,0:T(8,128)(2,1)}, bf16[192,1536]{1,0:T(8,128)(2,1)}, u32[]{:S(2)}, u32[]{:S(2)}) collective-permute-start(bf16[192,1536]{1,0:T(8,128)(2,1)} %get-tuple-element.440.refs_2_), channel_id=1, source_target_pairs={{0,8},{4,12},{8,16},{12,20},{16,24},{20,28},{24,0},{28,4},{1,9},{5... | collective-permute-start | bytes 1769480 | tf_op jit(solution)/shard_map/ppermute | solution.py:80
  105.4 29.4 %collective-permute-start.21 = (bf16[192,1536]{1,0:T(8,128)(2,1)}, bf16[192,1536]{1,0:T(8,128)(2,1)}, u32[]{:S(2)}, u32[]{:S(2)}) collective-permute-start(bf16[192,1536]{1,0:T(8,128)(2,1)} %collective-permute-done.12.refs_9_), channel_id=1, source_target_pairs={{0,4},{4,0},{8,12},{12,8},{16,20},{20,16},{24,28},{28,24},{1,5},{5... | collective-permute-start | bytes 1769480 | tf_op jit(solution)/shard_map/ppermute | solution.py:76
  106.6 28.3 %collective-permute-start.17 = (bf16[1024,192]{1,0:T(8,128)(2,1)}, bf16[1024,192]{1,0:T(8,128)(2,1)}, u32[]{:S(2)}, u32[]{:S(2)}) collective-permute-start(bf16[1024,192]{1,0:T(8,128)(2,1)} %get-tuple-element.368.refs_4_), channel_id=1, source_target_pairs={{0,2},{2,0},{1,3},{3,1},{4,6},{6,4},{5,7},{7,5},{8,10},{10,8},{9,1... | collective-permute-start | bytes 1179656 | tf_op jit(solution)/shard_map/ppermute | solution.py:47
  107.6 27.3 %collective-permute-start.18 = (bf16[1024,192]{1,0:T(8,128)(2,1)}, bf16[1024,192]{1,0:T(8,128)(2,1)}, u32[]{:S(2)}, u32[]{:S(2)}) collective-permute-start(bf16[1024,192]{1,0:T(8,128)(2,1)} %get-tuple-element.368.refs_4_), channel_id=1, source_target_pairs={{0,1},{1,0},{2,3},{3,2},{4,5},{5,4},{6,7},{7,6},{8,9},{9,8},{10,11... | collective-permute-start | bytes 1179656 | tf_op jit(solution)/shard_map/ppermute | solution.py:43
  134.8 27.8 %collective-permute-start.26 = (bf16[2,256,1536]{2,1,0:T(8,128)(2,1)}, bf16[2,256,1536]{2,1,0:T(8,128)(2,1)}, u32[]{:S(2)}, u32[]{:S(2)}) collective-permute-start(bf16[2,256,1536]{2,1,0:T(8,128)(2,1)} %collective-permute-done.19.refs_2_), channel_id=1, source_target_pairs={{0,1},{1,0},{2,3},{3,2},{4,5},{5,4},{6,7},{7,6},{8,9},{9,8},{10,11... | collective-permute-start | bytes 4718600 | tf_op jit(solution)/shard_map/ppermute | solution.py:43
  195.3 31.7 %collective-permute-start.32 = (bf16[192,1536]{1,0:T(8,128)(2,1)}, bf16[192,1536]{1,0:T(8,128)(2,1)S(1)}, u32[]{:S(2)}, u32[]{:S(2)}) collective-permute-start(bf16[192,1536]{1,0:T(8,128)(2,1)} %collective-permute-done.24.refs_6_), channel_id=1, source_target_pairs={{0,4},{4,0},{8,12},{12,8},{16,20},{20,16},{24,28},{28,24},{1,5},{5... | collective-permute-start | bytes 1769480 | tf_op jit(solution)/shard_map/ppermute | solution.py:76
  195.9 31.2 %collective-permute-start.33 = (bf16[192,1536]{1,0:T(8,128)(2,1)S(1)}, bf16[192,1536]{1,0:T(8,128)(2,1)S(1)}, u32[]{:S(2)}, u32[]{:S(2)}) collective-permute-start(bf16[192,1536]{1,0:T(8,128)(2,1)S(1)} %copy-done.54), channel_id=1, source_target_pairs={{0,4},{4,0},{8,12},{12,8},{16,20},{20,16},{24,28},{28,24},{1,5},{5... | collective-permute-start | bytes 1769480 | tf_op jit(solution)/shard_map/ppermute | solution.py:76
  254.1 20.7 %collective-permute-start.34 = (bf16[192,1536]{1,0:T(8,128)(2,1)S(1)}, bf16[192,1536]{1,0:T(8,128)(2,1)S(1)}, u32[]{:S(2)}, u32[]{:S(2)}) collective-permute-start(bf16[192,1536]{1,0:T(8,128)(2,1)S(1)} %get-tuple-element.434), channel_id=1, source_target_pairs={{0,4},{4,0},{8,12},{12,8},{16,20},{20,16},{24,28},{28,24},{1,5},{5... | collective-permute-start | bytes 1769480 | tf_op jit(solution)/shard_map/ppermute | solution.py:76
  275.6 24.8 %collective-permute-start.35 = (bf16[2,256,1536]{2,1,0:T(8,128)(2,1)}, bf16[2,256,1536]{2,1,0:T(8,128)(2,1)S(1)}, u32[]{:S(2)}, u32[]{:S(2)}) collective-permute-start(bf16[2,256,1536]{2,1,0:T(8,128)(2,1)} %bitcast.337), channel_id=1, source_target_pairs={{0,1},{1,0},{2,3},{3,2},{4,5},{5,4},{6,7},{7,6},{8,9},{9,8},{10,11... | collective-permute-start | bytes 4718600 | tf_op jit(solution)/shard_map/ppermute | solution.py:43
  278.6 21.8 %collective-permute-start.37 = (bf16[192,1536]{1,0:T(8,128)(2,1)}, bf16[192,1536]{1,0:T(8,128)(2,1)}, u32[]{:S(2)}, u32[]{:S(2)}) collective-permute-start(bf16[192,1536]{1,0:T(8,128)(2,1)} %add_convert_fusion.14), channel_id=1, source_target_pairs={{0,8},{4,12},{8,16},{12,20},{16,24},{20,28},{24,0},{28,4},{1,9},{5... | collective-permute-start | bytes 1769480 | tf_op jit(solution)/shard_map/ppermute | solution.py:80
  278.6 21.8 %collective-permute-start.36 = (bf16[192,1536]{1,0:T(8,128)(2,1)}, bf16[192,1536]{1,0:T(8,128)(2,1)}, u32[]{:S(2)}, u32[]{:S(2)}) collective-permute-start(bf16[192,1536]{1,0:T(8,128)(2,1)} %get-tuple-element.457), channel_id=1, source_target_pairs={{0,4},{4,0},{8,12},{12,8},{16,20},{20,16},{24,28},{28,24},{1,5},{5... | collective-permute-start | bytes 1769480 | tf_op jit(solution)/shard_map/ppermute | solution.py:76
  303.5 24.8 %collective-permute-start.42 = (bf16[192,1536]{1,0:T(8,128)(2,1)}, bf16[192,1536]{1,0:T(8,128)(2,1)}, u32[]{:S(2)}, u32[]{:S(2)}) collective-permute-start(bf16[192,1536]{1,0:T(8,128)(2,1)} %add_convert_fusion.13), channel_id=1, source_target_pairs={{0,8},{4,12},{8,16},{12,20},{16,24},{20,28},{24,0},{28,4},{1,9},{5... | collective-permute-start | bytes 1769480 | tf_op jit(solution)/shard_map/ppermute | solution.py:80
  305.2 39.0 %collective-permute-start.39 = (bf16[256,1536]{1,0:T(8,128)(2,1)}, bf16[256,1536]{1,0:T(8,128)(2,1)}, u32[]{:S(2)}, u32[]{:S(2)}) collective-permute-start(bf16[256,1536]{1,0:T(8,128)(2,1)} %fusion.34), channel_id=1, source_target_pairs={{0,2},{2,0},{1,3},{3,1},{4,6},{6,4},{5,7},{7,5},{8,10},{10,8},{9,1... | collective-permute-start | bytes 2359304 | tf_op jit(solution)/shard_map/ppermute | solution.py:47
  306.2 37.9 %collective-permute-start.38 = (bf16[2,256,1536]{2,1,0:T(8,128)(2,1)}, bf16[2,256,1536]{2,1,0:T(8,128)(2,1)}, u32[]{:S(2)}, u32[]{:S(2)}) collective-permute-start(bf16[2,256,1536]{2,1,0:T(8,128)(2,1)} %bitcast.332), channel_id=1, source_target_pairs={{0,1},{1,0},{2,3},{3,2},{4,5},{5,4},{6,7},{7,6},{8,9},{9,8},{10,11... | collective-permute-start | bytes 4718600 | tf_op jit(solution)/shard_map/ppermute | solution.py:43
  306.2 37.9 %collective-permute-start.40 = (bf16[2,256,1536]{2,1,0:T(8,128)(2,1)}, bf16[2,256,1536]{2,1,0:T(8,128)(2,1)}, u32[]{:S(2)}, u32[]{:S(2)}) collective-permute-start(bf16[2,256,1536]{2,1,0:T(8,128)(2,1)} %bitcast.335), channel_id=1, source_target_pairs={{0,1},{1,0},{2,3},{3,2},{4,5},{5,4},{6,7},{7,6},{8,9},{9,8},{10,11... | collective-permute-start | bytes 4718600 | tf_op jit(solution)/shard_map/ppermute | solution.py:43
  306.7 37.4 %collective-permute-start.43 = (bf16[2,256,1536]{2,1,0:T(8,128)(2,1)}, bf16[2,256,1536]{2,1,0:T(8,128)(2,1)}, u32[]{:S(2)}, u32[]{:S(2)}) collective-permute-start(bf16[2,256,1536]{2,1,0:T(8,128)(2,1)} %bitcast.334), channel_id=1, source_target_pairs={{0,1},{1,0},{2,3},{3,2},{4,5},{5,4},{6,7},{7,6},{8,9},{9,8},{10,11... | collective-permute-start | bytes 4718600 | tf_op jit(solution)/shard_map/ppermute | solution.py:43
  405.4 21.6 %collective-permute-start.55 = (bf16[256,1536]{1,0:T(8,128)(2,1)}, bf16[256,1536]{1,0:T(8,128)(2,1)}, u32[]{:S(2)}, u32[]{:S(2)}) collective-permute-start(bf16[256,1536]{1,0:T(8,128)(2,1)} %fusion.36), channel_id=1, source_target_pairs={{0,2},{2,0},{1,3},{3,1},{4,6},{6,4},{5,7},{7,5},{8,10},{10,8},{9,1... | collective-permute-start | bytes 2359304 | tf_op jit(solution)/shard_map/ppermute | solution.py:47
  407.4 22.5 %collective-permute-start.59 = (bf16[192,1536]{1,0:T(8,128)(2,1)}, bf16[192,1536]{1,0:T(8,128)(2,1)}, u32[]{:S(2)}, u32[]{:S(2)}) collective-permute-start(bf16[192,1536]{1,0:T(8,128)(2,1)} %add_convert_fusion.9), channel_id=1, source_target_pairs={{0,8},{4,12},{8,16},{12,20},{16,24},{20,28},{24,0},{28,4},{1,9},{5... | collective-permute-start | bytes 1769480 | tf_op jit(solution)/shard_map/ppermute | solution.py:80
  408.4 21.6 %collective-permute-start.57 = (bf16[8,48,1536]{2,1,0:T(8,128)(2,1)}, bf16[8,48,1536]{2,1,0:T(8,128)(2,1)}, u32[]{:S(2)}, u32[]{:S(2)}) collective-permute-start(bf16[8,48,1536]{2,1,0:T(8,128)(2,1)} %get-tuple-element.511), channel_id=1, source_target_pairs={{0,1},{1,0},{2,3},{3,2},{4,5},{5,4},{6,7},{7,6},{8,9},{9,8},{10,11... | collective-permute-start | bytes 3538952 | tf_op jit(solution)/shard_map/ppermute | solution.py:43
  408.4 21.6 %collective-permute-start.58 = (bf16[192,1536]{1,0:T(8,128)(2,1)}, bf16[192,1536]{1,0:T(8,128)(2,1)}, u32[]{:S(2)}, u32[]{:S(2)}) collective-permute-start(bf16[192,1536]{1,0:T(8,128)(2,1)} %get-tuple-element.512), channel_id=1, source_target_pairs={{0,4},{4,0},{8,12},{12,8},{16,20},{20,16},{24,28},{28,24},{1,5},{5... | collective-permute-start | bytes 1769480 | tf_op jit(solution)/shard_map/ppermute | solution.py:76
  409.9 20.0 %collective-permute-start.56 = (bf16[256,192]{1,0:T(8,128)(2,1)}, bf16[256,192]{1,0:T(8,128)(2,1)}, u32[]{:S(2)}, u32[]{:S(2)}) collective-permute-start(bf16[256,192]{1,0:T(8,128)(2,1)} %get-tuple-element.510), channel_id=1, source_target_pairs={{0,1},{1,0},{2,3},{3,2},{4,5},{5,4},{6,7},{7,6},{8,9},{9,8},{10,11... | collective-permute-start | bytes 294920 | tf_op jit(solution)/shard_map/ppermute | solution.py:43
  432.4 24.4 %collective-permute-start.62 = (bf16[192,1536]{1,0:T(8,128)(2,1)}, bf16[192,1536]{1,0:T(8,128)(2,1)}, u32[]{:S(2)}, u32[]{:S(2)}) collective-permute-start(bf16[192,1536]{1,0:T(8,128)(2,1)} %add_convert_fusion.8), channel_id=1, source_target_pairs={{0,8},{4,12},{8,16},{12,20},{16,24},{20,28},{24,0},{28,4},{1,9},{5... | collective-permute-start | bytes 1769480 | tf_op jit(solution)/shard_map/ppermute | solution.py:80
  435.1 23.8 %collective-permute-start.60 = (bf16[256,1536]{1,0:T(8,128)(2,1)}, bf16[256,1536]{1,0:T(8,128)(2,1)}, u32[]{:S(2)}, u32[]{:S(2)}) collective-permute-start(bf16[256,1536]{1,0:T(8,128)(2,1)} %fusion.37), channel_id=1, source_target_pairs={{0,2},{2,0},{1,3},{3,1},{4,6},{6,4},{5,7},{7,5},{8,10},{10,8},{9,1... | collective-permute-start | bytes 2359304 | tf_op jit(solution)/shard_map/ppermute | solution.py:47
  435.4 21.4 %collective-permute-start.61 = (bf16[192,1536]{1,0:T(8,128)(2,1)}, bf16[192,1536]{1,0:T(8,128)(2,1)}, u32[]{:S(2)}, u32[]{:S(2)}) collective-permute-start(bf16[192,1536]{1,0:T(8,128)(2,1)} %get-tuple-element.536), channel_id=1, source_target_pairs={{0,4},{4,0},{8,12},{12,8},{16,20},{20,16},{24,28},{28,24},{1,5},{5... | collective-permute-start | bytes 1769480 | tf_op jit(solution)/shard_map/ppermute | solution.py:76
  458.9 22.7 %collective-permute-start.63 = (bf16[192,1536]{1,0:T(8,128)(2,1)S(1)}, bf16[192,1536]{1,0:T(8,128)(2,1)}, u32[]{:S(2)}, u32[]{:S(2)}) collective-permute-start(bf16[192,1536]{1,0:T(8,128)(2,1)S(1)} %copy-done.28), channel_id=1, source_target_pairs={{0,2},{2,0},{1,3},{3,1},{4,6},{6,4},{5,7},{7,5},{8,10},{10,8},{9,1... | collective-permute-start | bytes 1769480 | tf_op jit(solution)/shard_map/ppermute | solution.py:47
  460.2 21.4 %collective-permute-start.65 = (bf16[192,1536]{1,0:T(8,128)(2,1)S(1)}, bf16[192,1536]{1,0:T(8,128)(2,1)}, u32[]{:S(2)}, u32[]{:S(2)}) collective-permute-start(bf16[192,1536]{1,0:T(8,128)(2,1)S(1)} %copy-done.28), channel_id=1, source_target_pairs={{0,1},{1,0},{2,3},{3,2},{4,5},{5,4},{6,7},{7,6},{8,9},{9,8},{10,11... | collective-permute-start | bytes 1769480 | tf_op jit(solution)/shard_map/ppermute | solution.py:43
  461.4 20.1 %collective-permute-start.66 = (bf16[48,1536]{1,0:T(8,128)(2,1)S(1)}, bf16[48,1536]{1,0:T(8,128)(2,1)}, u32[]{:S(2)}, u32[]{:S(2)}) collective-permute-start(bf16[48,1536]{1,0:T(8,128)(2,1)S(1)} %get-tuple-element.551), channel_id=1, source_target_pairs={{0,4},{4,0},{8,12},{12,8},{16,20},{20,16},{24,28},{28,24},{1,5},{5... | collective-permute-start | bytes 442376 | tf_op jit(solution)/shard_map/ppermute | solution.py:76
  484.0 28.2 %collective-permute-start.69 = (bf16[2,256,1536]{2,1,0:T(8,128)(2,1)}, bf16[2,256,1536]{2,1,0:T(8,128)(2,1)}, u32[]{:S(2)}, u32[]{:S(2)}) collective-permute-start(bf16[2,256,1536]{2,1,0:T(8,128)(2,1)} %bitcast.336), channel_id=1, source_target_pairs={{0,1},{1,0},{2,3},{3,2},{4,5},{5,4},{6,7},{7,6},{8,9},{9,8},{10,11... | collective-permute-start | bytes 4718600 | tf_op jit(solution)/shard_map/ppermute | solution.py:43
  484.0 29.0 %collective-permute-start.73 = (bf16[2,256,1536]{2,1,0:T(8,128)(2,1)}, bf16[2,256,1536]{2,1,0:T(8,128)(2,1)}, u32[]{:S(2)}, u32[]{:S(2)}) collective-permute-start(bf16[2,256,1536]{2,1,0:T(8,128)(2,1)} %bitcast.333), channel_id=1, source_target_pairs={{0,1},{1,0},{2,3},{3,2},{4,5},{5,4},{6,7},{7,6},{8,9},{9,8},{10,11... | collective-permute-start | bytes 4718600 | tf_op jit(solution)/shard_map/ppermute | solution.py:43
  532.3 23.2 %collective-permute-start.75 = (bf16[256,1536]{1,0:T(8,128)(2,1)S(1)}, bf16[256,1536]{1,0:T(8,128)(2,1)S(1)}, u32[]{:S(2)}, u32[]{:S(2)}) collective-permute-start(bf16[256,1536]{1,0:T(8,128)(2,1)S(1)} %fusion.38), channel_id=1, source_target_pairs={{0,2},{2,0},{1,3},{3,1},{4,6},{6,4},{5,7},{7,5},{8,10},{10,8},{9,1... | collective-permute-start | bytes 2359304 | tf_op jit(solution)/shard_map/ppermute | solution.py:47
  (157 other events, 1450.3 us)
